TPU v7x, 256 devices: a whole 4x4x8 slice. The times are simulated.
256 devices in a mesh: blk: 128 (over y_lo, x, z, core), pair: 2 (over y_hi).
Axes of the slice: x: 4, y: 4 (y_hi: 2, y_lo: 2; y = y_hi * 2 + y_lo), z: 8, core: 2. Of those that a mesh axis runs over, the one named last changes fastest.
Arguments:
- vertex: bfloat16 [128, 2048, 2048], P('blk', 'pair'), may hold values from -0.125 to 0.125
- left_phase: bfloat16 [128, 2048, 512], P('blk', 'pair'), may hold values from -6 to 6
- right_phase: bfloat16 [128, 2048, 512], P('blk'), may hold values from -6 to 6
- tiles: bfloat16 [512, 512, 512], P('blk'), may hold values from -0.25 to 0.25
- orders: int32 [128], P('blk'), may hold values from 512 to 2048, as said below
- momentum: int32 [512], replicated, may hold values from 0 to 63
- frequency: int32 [512], replicated, may hold values from 0 to 31
Outputs:
- suscept: bfloat16 [512, 512, 512], P('blk', 'pair')
- sigma: float32 [2048], P(('blk', 'pair'))
Inputs may be any that keep to these rules, and one draw needn't show every extreme that they name: `orders`: every order is at least 512 and at most 2048; some walker has order exactly 2048.
All inputs are finite; a program needn't handle non-finite values.
Results may differ from a plain program's by a relative error of at most 0.0075.
Values may be sent and summed in bfloat16 or wider, within the bound.
No kernel may reach another device: no remote copies, remote signals or barrier semaphores. Data moves between devices by JAX's collectives and lax.ppermute only.
A program may use at most 64 MiB of HBM per device.

v0:
```python
import math

import jax
import jax.numpy as jnp
from jax import lax
from jax.sharding import PartitionSpec as P

NMOM = 64
NFREQ = 32


def passed_along(value, axis, steps):
    count = lax.axis_size(axis)
    pairs = [(source, (source + steps) % count) for source in range(count)]
    return lax.ppermute(value, axis, pairs)


def transform_rows(vertex_rows, left_rows, right_full, live_rows, live_cols):
    masked = jnp.where(
        live_rows[:, None] & live_cols[None, :], vertex_rows, jnp.zeros_like(vertex_rows)
    )
    carried = jnp.dot(masked, right_full, preferred_element_type=jnp.float32).astype(jnp.bfloat16)
    return lax.dot_general(
        left_rows, carried, (((0,), (0,)), ((), ())), preferred_element_type=jnp.float32
    )


def per_device(vertex, left_phase, right_phase, tiles, orders, momentum, frequency):
    vertex_rows = vertex[0]
    left_rows = left_phase[0]
    right_full = right_phase[0]
    height = vertex_rows.shape[0]
    breadth = vertex_rows.shape[1]
    states = right_full.shape[1]
    member = lax.axis_index("pair")
    first_row = member * height
    order = orders[0]
    live_cols = jnp.arange(breadth, dtype=jnp.int32) < order
    row_ids = first_row + jnp.arange(height, dtype=jnp.int32)
    partial_value = transform_rows(vertex_rows, left_rows, right_full, row_ids < order, live_cols)
    scale = 1.0 / math.sqrt(breadth)
    green = (lax.psum(partial_value, "pair") * scale).astype(jnp.bfloat16)
    window = [green]
    moving = green
    for offset in range(2):
        moving = passed_along(moving, "blk", 1)
        window.append(moving)
    moving = green
    for offset in range(2):
        moving = passed_along(moving, "blk", -1)
        window.append(moving)
    half_states = states // 2
    first_state = member * half_states
    running = jnp.zeros((tiles.shape[0], half_states, states), jnp.float32)
    for walker_green in window:
        upper = lax.dynamic_slice_in_dim(walker_green, first_state, half_states, 0)
        inner = jnp.einsum("sa,tab->tsb", upper, tiles, preferred_element_type=jnp.float32).astype(
            jnp.bfloat16
        )
        running = running + jnp.einsum(
            "tsb,cb->tsc", inner, walker_green, preferred_element_type=jnp.float32
        )
    suscept = running * (1.0 / math.sqrt(states))
    summed = jnp.sum(suscept, axis=0)
    mom_rows = lax.dynamic_slice_in_dim(momentum, first_state, half_states, 0)
    onehot_mom = (mom_rows[:, None] == jnp.arange(NMOM, dtype=jnp.int32)[None, :]).astype(
        jnp.float32
    )
    onehot_freq = (frequency[:, None] == jnp.arange(NFREQ, dtype=jnp.int32)[None, :]).astype(
        jnp.float32
    )
    folded = jnp.dot(summed, onehot_freq, precision=lax.Precision.HIGHEST)
    cells = jnp.dot(onehot_mom.T, folded, precision=lax.Precision.HIGHEST)
    factor = 1.0 / math.sqrt(
        5.0 * tiles.shape[0] * lax.axis_size("blk") * states * states / (NMOM * NFREQ)
    )
    owned = lax.psum_scatter(
        (cells * factor).reshape(-1), ("blk", "pair"), scatter_dimension=0, tiled=True
    )
    return (suscept.astype(jnp.bfloat16), owned)


def solution(mesh):
    in_specs = (
        P("blk", "pair", None),
        P("blk", "pair", None),
        P("blk", None, None),
        P("blk", None, None),
        P("blk"),
        P(),
        P(),
    )
    out_specs = (P("blk", "pair", None), P(("blk", "pair")))
    return jax.shard_map(
        per_device, mesh=mesh, in_specs=in_specs, out_specs=out_specs, check_vma=False
    )
```

profile of v0, /device:TPU:1, one launch (start us, length us, event | category | flops | bytes accessed | tf_op | source)
XLA Modules:
  0.0 190.8 jit_solution(14871304014389715013)
XLA Ops:
  7.2 0.0 copy-start
  7.2 0.0 all-reduce.3.cloned.1.call-start
  8.0 7.0 %convolution_bitcast_fusion = f32[512,512]{0,1:T(8,128)} fusion(bf16[1,2048,512]{2,1,0:T(8,128)(2,1)} %param.9, bf16[1,1024,2048]{2,1,0:T(8,128)(2,1)} %param.7, pred[2048]{0:T(1024)(128)(4,1)S(1)} %iota_compare_fusion.4, pred[1024]{0:T(1024)(128)(4,1)S(1)} %add_compare_fusion, bf16[1,1024,512]{2,1,0:T(8,128)(2,1)} %param.8), kind=kOutput, calls=%fused_computation.23 | convolution fusion | flops 2689073152 | bytes 8391680 | tf_op jit(solution)/shard_map/dot_general | solution.py:23
  15.0 0.0 copy-start.2
  15.0 0.0 all-reduce.3.cloned.1.call-update
  15.0 57.2 %all-reduce.3.cloned.1.call-done = f32[512,512]{0,1:T(8,128)} async-done(((f32[512,512]{0,1:T(8,128)}), f32[512,512]{0,1:T(8,128)}) %all-reduce.3.cloned.1.call-update) | async-done | bytes 1048592 | tf_op jit(solution)/shard_map/psum | solution.py:42
  72.3 1.3 multiply_convert_fusion
  73.6 1.9 %collective-permute-start = (bf16[512,512]{0,1:T(8,128)(2,1)S(1)}, bf16[512,512]{0,1:T(8,128)(2,1)}, u32[]{:S(2)}, u32[]{:S(2)}) collective-permute-start(bf16[512,512]{0,1:T(8,128)(2,1)S(1)} %multiply_convert_fusion), channel_id=1, source_target_pairs={{0,2},{2,4},{4,6},{6,8},{8,10},{10,12},{12,14},{14,16},{16,18},{18... | collective-permute-start | bytes 1572872 | tf_op jit(solution)/shard_map/ppermute | solution.py:15
  75.5 0.0 collective-permute-start.2
  75.5 0.0 copy-done.2
  75.5 0.1 dynamic_slice.23
  75.6 0.0 copy-done
  75.6 2.6 %fusion.20 = f32[4,256,512]{2,1,0:T(8,128)} fusion(bf16[4,512,512]{2,1,0:T(8,128)(2,1)S(1)} %copy-done, bf16[512,512]{0,1:T(8,128)(2,1)S(1)} %multiply_convert_fusion, s32[]{:T(128)S(6)} %select_n.17), kind=kOutput, calls=%fused_computation.22 | convolution fusion | flops 1074266112 | bytes 4980740 | tf_op jit(solution)/shard_map/tsb,cb->tsc/dot_general | solution.py:60
  78.2 3.4 %collective-permute-done = bf16[512,512]{0,1:T(8,128)(2,1)} collective-permute-done((bf16[512,512]{0,1:T(8,128)(2,1)S(1)}, bf16[512,512]{0,1:T(8,128)(2,1)}, u32[]{:S(2)}, u32[]{:S(2)}) %collective-permute-start) | collective-permute-done | bytes 524320 | tf_op jit(solution)/shard_map/ppermute | solution.py:15
  81.7 2.6 %collective-permute-start.1 = (bf16[512,512]{0,1:T(8,128)(2,1)}, bf16[512,512]{0,1:T(8,128)(2,1)}, u32[]{:S(2)}, u32[]{:S(2)}) collective-permute-start(bf16[512,512]{0,1:T(8,128)(2,1)} %collective-permute-done), channel_id=1, source_target_pairs={{0,2},{2,4},{4,6},{6,8},{8,10},{10,12},{12,14},{14,16},{16,18},{18... | collective-permute-start | bytes 1572872 | tf_op jit(solution)/shard_map/ppermute | solution.py:15
  84.2 0.3 collective-permute-done.2
  84.5 2.8 %collective-permute-start.3 = (bf16[512,512]{0,1:T(8,128)(2,1)}, bf16[512,512]{0,1:T(8,128)(2,1)S(1)}, u32[]{:S(2)}, u32[]{:S(2)}) collective-permute-start(bf16[512,512]{0,1:T(8,128)(2,1)} %collective-permute-done.2), channel_id=1, source_target_pairs={{0,254},{2,0},{4,2},{6,4},{8,6},{10,8},{12,10},{14,12},{16,14},{18... | collective-permute-start | bytes 1572872 | tf_op jit(solution)/shard_map/ppermute | solution.py:15
  87.3 3.7 %fusion.17 = f32[4,256,512]{2,1,0:T(8,128)} fusion(bf16[4,512,512]{2,1,0:T(8,128)(2,1)S(1)} %copy-done, bf16[512,512]{0,1:T(8,128)(2,1)} %collective-permute-done.2, s32[]{:T(128)S(6)} %select_n.17), kind=kOutput, calls=%fused_computation.19 | convolution fusion | flops 1074266112 | bytes 4980740 | tf_op jit(solution)/shard_map/tsb,cb->tsc/dot_general | solution.py:60
  91.0 3.7 %fusion.19 = f32[4,256,512]{2,1,0:T(8,128)} fusion(bf16[4,512,512]{2,1,0:T(8,128)(2,1)S(1)} %copy-done, bf16[512,512]{0,1:T(8,128)(2,1)} %collective-permute-done, s32[]{:T(128)S(6)} %select_n.17), kind=kOutput, calls=%fused_computation.21 | convolution fusion | flops 1074266112 | bytes 4980740 | tf_op jit(solution)/shard_map/tsb,cb->tsc/dot_general | solution.py:60
  94.7 0.0 collective-permute-done.1
  94.7 3.8 %fusion.18 = f32[4,256,512]{2,1,0:T(8,128)} fusion(bf16[4,512,512]{2,1,0:T(8,128)(2,1)S(1)} %copy-done, bf16[512,512]{0,1:T(8,128)(2,1)} %collective-permute-done.1, s32[]{:T(128)S(6)} %select_n.17), kind=kOutput, calls=%fused_computation.20 | convolution fusion | flops 1074266112 | bytes 4980740 | tf_op jit(solution)/shard_map/tsb,cb->tsc/dot_general | solution.py:60
  98.5 0.0 copy-start.1
  98.5 0.0 collective-permute-done.3
  98.5 6.0 %fusion.66 = (f32[256,512]{1,0:T(8,128)S(1)}, bf16[4,256,512]{2,1,0:T(8,128)(2,1)}) fusion(bf16[512,512]{0,1:T(8,128)(2,1)S(1)} %collective-permute-done.3, bf16[4,512,512]{2,1,0:T(8,128)(2,1)S(1)} %copy-done, s32[]{:T(128)S(6)} %select_n.17, f32[4,256,512]{2,1,0:T(8,128)} %fusion.17, f32[4,256,512]{2,1,0:T(8,128)} %fusion.18, f32[4,256,512]{2,1,0:T(8,128)} %fusion.20, ...), kind=kOutput, calls=%fused_computation.55 | convolution fusion | flops 1077805056 | bytes 12845060 | tf_op jit(solution)/shard_map/tsb,cb->tsc/dot_general | solution.py:60
  104.5 0.0 copy-done.1
  104.5 0.4 fusion.51
  105.0 0.2 convolution_multiply_fusion
  105.2 0.1 copy.30
  105.3 0.1 reshape.62
  105.4 77.9 %all-reduce = f32[2048]{0:T(1024)S(1)} all-reduce(f32[2048]{0:T(1024)S(1)} %reshape.62), channel_id=2, replica_groups=mesh['blk'=128,'pair'=2] {'blk','pair'}, use_global_device_ids=true, to_apply=%region_2.3.clone | all-reduce | flops 2048 | bytes 16384
  183.3 0.6 dynamic-slice
  (2 shorter events, 0.0 us)
Async XLA Ops:
  7.2 68.5 %copy-start = (bf16[4,512,512]{2,1,0:T(8,128)(2,1)S(1)}, bf16[4,512,512]{2,1,0:T(8,128)(2,1)}, u32[]{:S(2)}) copy-start(bf16[4,512,512]{2,1,0:T(8,128)(2,1)} %param.10) | copy-start | bytes 6291460
  7.2 65.1 %all-reduce.3.cloned.1.call-start = ((), (), s32[]{:S(2)}) async-start(), calls=%async_computation | async-start | bytes 2097152 | tf_op jit(solution)/shard_map/psum | solution.py:42
  15.0 60.5 %copy-start.2 = (s32[512]{0:T(512)S(1)}, s32[512]{0:T(512)}, u32[]{:S(2)}) copy-start(s32[512]{0:T(512)} %param.12) | copy-start | bytes 6148
  73.6 8.0 %collective-permute-start = (bf16[512,512]{0,1:T(8,128)(2,1)S(1)}, bf16[512,512]{0,1:T(8,128)(2,1)}, u32[]{:S(2)}, u32[]{:S(2)}) collective-permute-start(bf16[512,512]{0,1:T(8,128)(2,1)S(1)} %multiply_convert_fusion), channel_id=1, source_target_pairs={{0,2},{2,4},{4,6},{6,8},{8,10},{10,12},{12,14},{14,16},{16,18},{18... | collective-permute-start | bytes 1572872 | tf_op jit(solution)/shard_map/ppermute | solution.py:15
  75.5 9.0 %collective-permute-start.2 = (bf16[512,512]{0,1:T(8,128)(2,1)S(1)}, bf16[512,512]{0,1:T(8,128)(2,1)}, u32[]{:S(2)}, u32[]{:S(2)}) collective-permute-start(bf16[512,512]{0,1:T(8,128)(2,1)S(1)} %multiply_convert_fusion), channel_id=1, source_target_pairs={{0,254},{2,0},{4,2},{6,4},{8,6},{10,8},{12,10},{14,12},{16,14},{18... | collective-permute-start | bytes 1572872 | tf_op jit(solution)/shard_map/ppermute | solution.py:15
  81.7 13.1 %collective-permute-start.1 = (bf16[512,512]{0,1:T(8,128)(2,1)}, bf16[512,512]{0,1:T(8,128)(2,1)}, u32[]{:S(2)}, u32[]{:S(2)}) collective-permute-start(bf16[512,512]{0,1:T(8,128)(2,1)} %collective-permute-done), channel_id=1, source_target_pairs={{0,2},{2,4},{4,6},{6,8},{8,10},{10,12},{12,14},{14,16},{16,18},{18... | collective-permute-start | bytes 1572872 | tf_op jit(solution)/shard_map/ppermute | solution.py:15
  84.5 14.0 %collective-permute-start.3 = (bf16[512,512]{0,1:T(8,128)(2,1)}, bf16[512,512]{0,1:T(8,128)(2,1)S(1)}, u32[]{:S(2)}, u32[]{:S(2)}) collective-permute-start(bf16[512,512]{0,1:T(8,128)(2,1)} %collective-permute-done.2), channel_id=1, source_target_pairs={{0,254},{2,0},{4,2},{6,4},{8,6},{10,8},{12,10},{14,12},{16,14},{18... | collective-permute-start | bytes 1572872 | tf_op jit(solution)/shard_map/ppermute | solution.py:15
  98.5 6.0 %copy-start.1 = (s32[512]{0:T(512)S(1)}, s32[512]{0:T(512)}, u32[]{:S(2)}) copy-start(s32[512]{0:T(512)} %param.13) | copy-start | bytes 6148
Sparse Core Ops, SparseCore 0:
  15.1 57.0 all-reduce.2
where the time goes:
time: 191 us
  blocking collectives  77.9 us (41%)
  waiting for transfers between devices  61 us (32%)
  matrix products  27.5 us (14%)
  between operations  14.9 us (8%)
  starting transfers between devices  7.31 us (4%)
    unnamed x1, blocking collectives  77.9 us
    psum x1, waiting for transfers between devices, per_device(): green = (lax.psum(partial_value, 'pair') * scale).astype(jnp.bfloat16)  57.2 us
    dot_general x5, matrix products, per_device(): jnp.einsum('tsb,cb->tsc', inner, walker_green, preferred_element_type=jnp...  19.8 us
    ppermute x4, starting transfers between devices, passed_along(): return lax.ppermute(value, axis, pairs)  7.27 us
    dot_general x1, matrix products, transform_rows(): lax.dot_general(left_rows, carried, (((0,), (0,)), ((), ())), preferred_e...  6.95 us
  transfers between devices with their start and end apart: 5, of which 3 were waited for; matrix products, arithmetic and copies ran while one was open for 7% of the time, Pallas kernels for 0%

commit v1 on v0

v1 whole, which is shorter than its diff:
```python
import functools
import math

import jax
import jax.numpy as jnp
from jax import lax
from jax.experimental import pallas as pl
from jax.experimental.pallas import tpu as pltpu
from jax.sharding import PartitionSpec as P

NMOM = 64
NFREQ = 32
BOTH = ("blk", "pair")
F32 = jnp.float32
BF16 = jnp.bfloat16
CHUNKS = 4
MIB = 1024 * 1024


def split_dot(left, right, dims):
    def halves(value):
        high = value.astype(BF16)
        return high, (value - high.astype(F32)).astype(BF16)

    (a_high, a_low), (b_high, b_low) = halves(left), halves(right)
    dot = functools.partial(lax.dot_general, dimension_numbers=(dims, ((), ())), preferred_element_type=F32)
    return dot(a_high, b_high) + dot(a_high, b_low) + dot(a_low, b_high)


def partial_kernel(
    scale, order_ref, vertex_hbm, right_hbm, left_hbm, exact_ref, sent_ref,
    vertex, right, left, total, sems,
):
    order = order_ref[0]
    first_row = lax.axis_index("pair") * total.shape[0]
    depth, states = right.shape[1:]
    copies = []
    for k in range(CHUNKS):
        span = pl.ds(k * depth, depth)
        copies.append(
            (
                pltpu.make_async_copy(right_hbm.at[span, :], right.at[k], sems.at[2 * k]),
                pltpu.make_async_copy(vertex_hbm.at[:, span], vertex.at[k], sems.at[2 * k + 1]),
            )
        )
    left_copy = pltpu.make_async_copy(left_hbm, left, sems.at[2 * CHUNKS])
    for pieces in copies:
        for copy in pieces:
            copy.start()
    left_copy.start()
    for k, pieces in enumerate(copies):
        for copy in pieces:
            copy.wait()

        @pl.when(order < (k + 1) * depth)
        def _():
            rows = lax.broadcasted_iota(jnp.int32, (depth, states), 0)
            right[k] = jnp.where(rows < order - k * depth, right[k], jnp.zeros_like(right[k]))

        product = jnp.dot(vertex[k], right[k], preferred_element_type=F32)
        if k == 0:
            total[...] = product
        else:
            total[...] += product
    left_copy.wait()
    live = lax.broadcasted_iota(jnp.int32, total.shape, 0) < order - first_row
    carried = jnp.where(live, total[...], 0.0).astype(BF16)
    green = (
        lax.dot_general(
            left[...], carried, (((0,), (0,)), ((), ())), preferred_element_type=F32
        )
        * scale
    )
    exact_ref[...] = green
    sent_ref[...] = green.astype(BF16)


def partial_green(order, vertex, right, left):
    height, breadth = vertex.shape
    states = right.shape[1]
    depth = breadth // CHUNKS
    hbm = pl.BlockSpec(memory_space=pltpu.HBM)
    vmem = pl.BlockSpec(memory_space=pltpu.VMEM)
    return pl.pallas_call(
        functools.partial(partial_kernel, 1.0 / math.sqrt(breadth)),
        in_specs=[pl.BlockSpec(memory_space=pltpu.SMEM), hbm, hbm, hbm],
        out_specs=[vmem] * 2,
        out_shape=[
            jax.ShapeDtypeStruct((states, states), F32),
            jax.ShapeDtypeStruct((states, states), BF16),
        ],
        scratch_shapes=[
            pltpu.VMEM((CHUNKS, height, depth), BF16),
            pltpu.VMEM((CHUNKS, depth, states), BF16),
            pltpu.VMEM((height, states), BF16),
            pltpu.VMEM((height, states), F32),
            pltpu.SemaphoreType.DMA((2 * CHUNKS + 1,)),
        ],
        compiler_params=pltpu.CompilerParams(vmem_limit_bytes=60 * MIB),
        cost_estimate=pl.CostEstimate(
            flops=2 * height * states * (breadth + states),
            bytes_accessed=2 * (height * breadth + breadth * states + height * states),
            transcendentals=0,
        ),
        name="partial_green",
    )(order, vertex, right, left)


def green_kernel(exact_ref, got_ref, green_ref):
    green_ref[...] = (exact_ref[...] + got_ref[...].astype(F32)).astype(BF16)


def whole_green(exact, got):
    vmem = pl.BlockSpec(memory_space=pltpu.VMEM)
    return pl.pallas_call(
        green_kernel,
        in_specs=[vmem] * 2,
        out_specs=vmem,
        out_shape=jax.ShapeDtypeStruct(exact.shape, BF16),
        compiler_params=pltpu.CompilerParams(vmem_limit_bytes=16 * MIB),
        cost_estimate=pl.CostEstimate(
            flops=exact.size, bytes_accessed=8 * exact.size, transcendentals=0
        ),
        name="whole_green",
    )(exact, got)


def sigma_kernel(factor, walkers, sum_ref, mom_ref, freq_ref, *refs):
    greens, (out_ref, stacked, left, right) = refs[:walkers], refs[walkers:]
    half, states = sum_ref.shape
    pick_mom = (lax.broadcasted_iota(jnp.int32, (NMOM, states), 0) == mom_ref[...]).astype(BF16)
    pick_freq = (lax.broadcasted_iota(jnp.int32, (NFREQ, states), 0) == freq_ref[...]).astype(BF16)
    first = pl.multiple_of(lax.axis_index("pair") * half, half)
    for u, ref in enumerate(greens):
        stacked[u * NMOM : (u + 1) * NMOM, :] = jnp.dot(
            pick_mom, ref[:, pl.ds(first, half)], preferred_element_type=F32
        )
        right[:, u * states : (u + 1) * states] = jnp.dot(
            pick_freq, ref[...], preferred_element_type=F32
        )
    folded = split_dot(stacked[...], sum_ref[...], ((1,), (0,)))
    for u in range(walkers):
        left[:, u * states : (u + 1) * states] = folded[u * NMOM : (u + 1) * NMOM]
    cells = split_dot(left[...], right[...], ((1,), (1,)))
    owners, width = out_ref.shape
    fold = NFREQ // width
    owner = lax.broadcasted_iota(jnp.int32, (owners, NMOM), 0)
    column = lax.broadcasted_iota(jnp.int32, (owners, NMOM), 1)
    spread = jnp.dot(
        (owner // fold == column).astype(F32),
        cells * factor,
        precision=lax.Precision.HIGHEST,
        preferred_element_type=F32,
    )
    turn = lax.broadcasted_iota(jnp.int32, (owners, width), 0) % fold
    result = jnp.zeros((owners, width), F32)
    for part in range(fold):
        result = jnp.where(turn == part, spread[:, part * width : (part + 1) * width], result)
    out_ref[...] = result


def sigma_cells(factor, tile_sum, greens, momentum, frequency, owners):
    width = NMOM * NFREQ // owners
    states = tile_sum.shape[1]
    vmem = pl.BlockSpec(memory_space=pltpu.VMEM)
    return pl.pallas_call(
        functools.partial(sigma_kernel, factor, len(greens)),
        in_specs=[vmem] * (3 + len(greens)),
        out_specs=vmem,
        out_shape=jax.ShapeDtypeStruct((owners, width), F32),
        scratch_shapes=[
            pltpu.VMEM((len(greens) * NMOM, states // 2), F32),
            pltpu.VMEM((NMOM, len(greens) * states), F32),
            pltpu.VMEM((NFREQ, len(greens) * states), F32),
        ],
        compiler_params=pltpu.CompilerParams(vmem_limit_bytes=16 * MIB),
        cost_estimate=pl.CostEstimate(flops=400_000_000, bytes_accessed=1_600_000, transcendentals=0),
        name="sigma_cells",
    )(tile_sum, momentum[None, :], frequency[None, :], *greens)


def chi_kernel(walkers, scale, *refs):
    greens, tile_ref, rest = refs[:walkers], refs[walkers], refs[walkers + 1 :]
    out_ref = rest[-1]
    half = out_ref.shape[1]
    first = pl.multiple_of(lax.axis_index("pair") * half, half)
    tile = tile_ref[0]
    total = None if len(rest) == 1 else rest[0][0]
    for green in greens:
        upper = green[pl.ds(first, half), :]
        inner = jnp.dot(upper, tile, preferred_element_type=F32).astype(BF16)
        term = lax.dot_general(
            inner, green[...], (((1,), (1,)), ((), ())), preferred_element_type=F32
        )
        total = term if total is None else total + term
    out_ref[0] = (total * scale).astype(out_ref.dtype)


def chi_terms(greens, tiles, running, scale, dtype, limit):
    count, states, _ = tiles.shape
    half = states // 2
    extra = [] if running is None else [running]
    whole = pl.BlockSpec((states, states), lambda t: (0, 0))
    rows = pl.BlockSpec((1, half, states), lambda t: (t, 0, 0))
    return pl.pallas_call(
        functools.partial(chi_kernel, len(greens), scale),
        grid=(count,),
        in_specs=[whole] * len(greens)
        + [pl.BlockSpec((1, states, states), lambda t: (t, 0, 0))]
        + [rows] * len(extra),
        out_specs=rows,
        out_shape=jax.ShapeDtypeStruct((count, half, states), dtype),
        compiler_params=pltpu.CompilerParams(vmem_limit_bytes=limit * MIB),
        cost_estimate=pl.CostEstimate(
            flops=len(greens) * count * 4 * half * states * states,
            bytes_accessed=2 * states * states * (count + len(greens)) + 4 * count * half * states,
            transcendentals=0,
        ),
        name="chi_terms",
    )(*greens, tiles, *extra)


def moves(mesh_shape):
    blk, pair = mesh_shape

    def flat(rule):
        return [(b * pair + p, rule(b, p)) for b in range(blk) for p in range(pair)]

    other = flat(lambda b, p: b * pair + (p + 1) % pair)
    core = flat(lambda b, p: (b ^ 1) * pair + p)

    def along(even, odd):
        return flat(lambda b, p: ((b + (odd if b % 2 else even)) % blk) * pair + p)

    return other, core, along(2, -2), along(-2, 2)


def send(value, pairs):
    return lax.ppermute(value, BOTH, pairs)


def per_device(vertex, left_phase, right_phase, tiles, orders, momentum, frequency):
    states = right_phase.shape[2]
    half = states // 2
    blk, pair = lax.axis_size("blk"), lax.axis_size("pair")
    other, core, outward, inward = moves((blk, pair))

    with jax.named_scope("green"):
        exact, sent = partial_green(orders, vertex[0], right_phase[0], left_phase[0])
        received = send(sent, other)
        own_rows = lax.dynamic_slice_in_dim(tiles, lax.axis_index("pair") * half, half, 1)
        tile_sum = jnp.sum(own_rows.astype(F32), axis=0)
        received, tile_sum = lax.optimization_barrier((received, tile_sum))
        green = whole_green(exact, received)

    with jax.named_scope("window"):
        green_core = send(green, core)
        green_in = send(green, inward)
        green_out = send(green, outward)
        running = chi_terms([green, green_core], tiles, None, 1.0, F32, 24)
        running, green_in = lax.optimization_barrier((running, green_in))
        green_last = send(green_in, core)
        far = [green_in, green_out, green_last]

    with jax.named_scope("sigma"):
        factor = 1.0 / math.sqrt(
            5.0 * tiles.shape[0] * blk * states * states / (NMOM * NFREQ)
        ) / math.sqrt(states)
        cells = sigma_cells(
            factor, tile_sum, [green, green_core] + far, momentum, frequency, blk * pair
        )
        running, cells = lax.optimization_barrier((running, cells))
        spread = lax.all_to_all(cells, BOTH, 0, 0, tiled=True)

    with jax.named_scope("chi"):
        suscept = chi_terms(far, tiles, running, 1.0 / math.sqrt(states), BF16, 60)
        suscept, spread = lax.optimization_barrier((suscept, spread))
        owned = jnp.sum(spread, axis=0)
    return suscept, owned


def solution(mesh):
    in_specs = (
        P("blk", "pair", None),
        P("blk", "pair", None),
        P("blk", None, None),
        P("blk", None, None),
        P("blk"),
        P(),
        P(),
    )
    out_specs = (P("blk", "pair", None), P(("blk", "pair")))
    return jax.shard_map(
        per_device, mesh=mesh, in_specs=in_specs, out_specs=out_specs, check_vma=False
    )
```

time: 191 us -> 75.6 us (0.40)
  blocking collectives: 77.9 us -> 0 us
  waiting for transfers between devices: 61 us -> 19.9 us
  matrix products: 27.5 us -> 0 us
  starting transfers between devices: 7.31 us -> 31.2 us
  Pallas kernels: 0 us -> 20.8 us
  between operations: 14.9 us -> 1.38 us
    unnamed x1 -> x0, blocking collectives: 77.9 us -> none
    psum x1 -> x0, waiting for transfers between devices: 57.2 us -> none  [per_device(): green = (lax.psum(partial_value, 'pair') * scale).astype(jnp.bfloat16)]
    dot_general x8 -> x0, matrix products: 27.5 us -> none  [the longest x5 19.8 us: per_device(): jnp.einsum('tsb,cb->tsc', inner, walker_green, preferred_element_type=jnp...]
    pallas_call x0 -> x5, Pallas kernels: none -> 20.8 us  [the longest x2 10.6 us: chi_terms(): pl.pallas_call(functools.partial(chi_kernel, len(greens), scale), grid=(c...]
    ppermute x4 -> x5, starting transfers between devices: 7.27 us -> 20.6 us  [send(): return lax.ppermute(value, BOTH, pairs)]
    all_to_all x0 -> x1, starting transfers between devices: none -> 10.6 us  [per_device(): spread = lax.all_to_all(cells, BOTH, 0, 0, tiled=True)]
    ppermute x4 -> x5, waiting for transfers between devices: 3.73 us -> 14.3 us  [send(): return lax.ppermute(value, BOTH, pairs)]
    all_to_all x0 -> x1, waiting for transfers between devices: none -> 5.61 us  [per_device(): spread = lax.all_to_all(cells, BOTH, 0, 0, tiled=True)]
  transfers between devices with their start and end apart: 5 -> 6, of which waited for: 3 -> 4; matrix products, arithmetic and copies ran while one was open for 7% -> 0% of each run, Pallas kernels for 0% -> 14%
where the time goes in v1:
time: 75.6 us; the launch traced here: 75.3 us
  starting transfers between devices  31.2 us (41%)
  Pallas kernels  20.8 us (28%)
  waiting for transfers between devices  19.9 us (26%)
  between operations  1.38 us (2%)
  local copies, waits for them, and re-layouts  1.36 us (2%)
    ppermute x5, starting transfers between devices, send(): return lax.ppermute(value, BOTH, pairs)  20.6 us
    ppermute x5, waiting for transfers between devices, send(): return lax.ppermute(value, BOTH, pairs)  14.3 us
    pallas_call x2, Pallas kernels, chi_terms(): pl.pallas_call(functools.partial(chi_kernel, len(greens), scale), grid=(c...  10.6 us
    all_to_all x1, starting transfers between devices, per_device(): spread = lax.all_to_all(cells, BOTH, 0, 0, tiled=True)  10.6 us
    pallas_call x1, Pallas kernels, partial_green(): pl.pallas_call(functools.partial(partial_kernel, 1.0 / math.sqrt(breadth)...  6.14 us
    all_to_all x1, waiting for transfers between devices, per_device(): spread = lax.all_to_all(cells, BOTH, 0, 0, tiled=True)  5.61 us
    pallas_call x1, Pallas kernels, sigma_cells(): pl.pallas_call(functools.partial(sigma_kernel, factor, len(greens)), in_s...  2.92 us
  transfers between devices with their start and end apart: 6, of which 4 were waited for; matrix products, arithmetic and copies ran while one was open for 0% of the time, Pallas kernels for 14%

profile of v1, /device:TPU:1, one launch (start us, length us, event | category | flops | bytes accessed | tf_op | source)
XLA Modules:
  0.0 75.3 jit_solution(11333409479202742573)
XLA Ops:
  1.3 0.0 copy-start.4
  1.3 6.1 %partial_green.1 = (f32[512,512]{1,0:T(8,128)}, bf16[512,512]{1,0:T(8,128)(2,1)}) custom-call(s32[1]{0:T(128)S(6)} %copy.10.order_ref, bf16[1024,2048]{1,0:T(8,128)(2,1)} %bitcast.12, bf16[2048,512]{1,0:T(8,128)(2,1)} %bitcast.13, bf16[1024,512]{1,0:T(8,128)(2,1)} %bitcast.14), custom_call_target="tpu_custom_call" | custom-call | flops 2684354560 | bytes 7340032 | tf_op jit(solution)/shard_map/green/partial_green/pallas_call | solution.py:84
  7.4 0.0 copy-start
  7.4 3.8 %collective-permute-start = (bf16[512,512]{1,0:T(8,128)(2,1)}, bf16[512,512]{1,0:T(8,128)(2,1)}, u32[]{:S(2)}, u32[]{:S(2)}) collective-permute-start(bf16[512,512]{1,0:T(8,128)(2,1)} %get-tuple-element.13), channel_id=1, source_target_pairs={{0,1},{1,0},{2,3},{3,2},{4,5},{5,4},{6,7},{7,6},{8,9},{9,8},{10,11... | collective-permute-start | bytes 1572872 | tf_op jit(solution)/shard_map/green/ppermute | solution.py:239
  11.3 0.0 copy-done.4
  11.3 0.1 convert_reduce_fusion.sum_ref
  11.4 10.8 %collective-permute-done.got_ref = bf16[512,512]{1,0:T(8,128)(2,1)} collective-permute-done((bf16[512,512]{1,0:T(8,128)(2,1)}, bf16[512,512]{1,0:T(8,128)(2,1)}, u32[]{:S(2)}, u32[]{:S(2)}) %collective-permute-start) | collective-permute-done | bytes 524320 | tf_op jit(solution)/shard_map/green/ppermute | solution.py:239
  22.2 0.0 copy-done
  22.2 1.1 %whole_green.1.refs_0_ = bf16[512,512]{1,0:T(8,128)(2,1)S(1)} custom-call(f32[512,512]{1,0:T(8,128)S(1)} %copy-done, bf16[512,512]{1,0:T(8,128)(2,1)} %collective-permute-done.got_ref), custom_call_target="tpu_custom_call" | custom-call | flops 262144 | bytes 2097152 | tf_op jit(solution)/shard_map/green/whole_green/pallas_call | solution.py:115
  23.3 0.0 copy-start.5
  23.3 0.0 copy-start.6
  23.3 2.4 %collective-permute-start.1 = (bf16[512,512]{1,0:T(8,128)(2,1)S(1)}, bf16[512,512]{1,0:T(8,128)(2,1)S(1)}, u32[]{:S(2)}, u32[]{:S(2)}) collective-permute-start(bf16[512,512]{1,0:T(8,128)(2,1)S(1)} %whole_green.1.refs_0_), channel_id=1, source_target_pairs={{0,2},{1,3},{2,0},{3,1},{4,6},{5,7},{6,4},{7,5},{8,10},{9,11},{10,... | collective-permute-start | bytes 1572872 | tf_op jit(solution)/shard_map/window/ppermute | solution.py:239
  25.7 1.7 %collective-permute-start.2 = (bf16[512,512]{1,0:T(8,128)(2,1)S(1)}, bf16[512,512]{1,0:T(8,128)(2,1)S(1)}, u32[]{:S(2)}, u32[]{:S(2)}) collective-permute-start(bf16[512,512]{1,0:T(8,128)(2,1)S(1)} %whole_green.1.refs_0_), channel_id=1, source_target_pairs={{0,252},{1,253},{2,6},{3,7},{4,0},{5,1},{6,10},{7,11},{8,4},{9,5},... | collective-permute-start | bytes 1572872 | tf_op jit(solution)/shard_map/window/ppermute | solution.py:239
  27.4 7.1 %collective-permute-start.3 = (bf16[512,512]{1,0:T(8,128)(2,1)S(1)}, bf16[512,512]{1,0:T(8,128)(2,1)S(1)}, u32[]{:S(2)}, u32[]{:S(2)}) collective-permute-start(bf16[512,512]{1,0:T(8,128)(2,1)S(1)} %whole_green.1.refs_0_), channel_id=1, source_target_pairs={{0,4},{1,5},{2,254},{3,255},{4,8},{5,9},{6,2},{7,3},{8,12},{9,13},... | collective-permute-start | bytes 1572872 | tf_op jit(solution)/shard_map/window/ppermute | solution.py:239
  34.5 0.0 collective-permute-done.1.refs_1_
  34.5 3.2 %chi_terms.2.refs_4_ = f32[4,256,512]{2,1,0:T(8,128)S(1)} custom-call(bf16[512,512]{1,0:T(8,128)(2,1)S(1)} %whole_green.1.refs_0_, bf16[512,512]{1,0:T(8,128)(2,1)S(1)} %collective-permute-done.1.refs_1_, bf16[4,512,512]{2,1,0:T(8,128)(2,1)S(1)} %copy-done.4), custom_call_target="tpu_custom_call" | custom-call | flops 2147483648 | bytes 5242880 | tf_op jit(solution)/shard_map/window/chi_terms/pallas_call | solution.py:205
  37.7 0.0 copy-start.7
  37.7 1.3 %copy-done.7 = f32[4,256,512]{2,1,0:T(8,128)} copy-done((f32[4,256,512]{2,1,0:T(8,128)}, f32[4,256,512]{2,1,0:T(8,128)S(1)}, u32[]{:S(2)}) %copy-start.7) | copy-done | bytes 2097176
  39.0 2.0 %collective-permute-done.2.refs_2_.refs_0_ = bf16[512,512]{1,0:T(8,128)(2,1)S(1)} collective-permute-done((bf16[512,512]{1,0:T(8,128)(2,1)S(1)}, bf16[512,512]{1,0:T(8,128)(2,1)S(1)}, u32[]{:S(2)}, u32[]{:S(2)}) %collective-permute-start.2) | collective-permute-done | bytes 524320 | tf_op jit(solution)/shard_map/window/ppermute | solution.py:239
  41.1 0.0 copy-start.1
  41.1 5.6 %collective-permute-start.4 = (bf16[512,512]{1,0:T(8,128)(2,1)S(1)}, bf16[512,512]{1,0:T(8,128)(2,1)S(1)}, u32[]{:S(2)}, u32[]{:S(2)}) collective-permute-start(bf16[512,512]{1,0:T(8,128)(2,1)S(1)} %collective-permute-done.2.refs_2_.refs_0_), channel_id=1, source_target_pairs={{0,2},{1,3},{2,0},{3,1},{4,6},{5,7},{6,4},{7,5},{8,10},{9,11},{10,... | collective-permute-start | bytes 1572872 | tf_op jit(solution)/shard_map/window/ppermute | solution.py:239
  46.7 0.0 collective-permute-done.3.refs_3_.refs_1_
  46.7 0.0 copy-start.2
  46.7 1.5 %collective-permute-done.4.refs_4_.refs_2_ = bf16[512,512]{1,0:T(8,128)(2,1)S(1)} collective-permute-done((bf16[512,512]{1,0:T(8,128)(2,1)S(1)}, bf16[512,512]{1,0:T(8,128)(2,1)S(1)}, u32[]{:S(2)}, u32[]{:S(2)}) %collective-permute-start.4) | collective-permute-done | bytes 524320 | tf_op jit(solution)/shard_map/window/ppermute | solution.py:239
  48.2 0.0 copy-start.3
  48.2 0.0 copy-done.5
  48.2 0.0 copy-done.6
  48.2 2.9 %sigma_cells.1 = f32[256,8]{1,0:T(8,128)} custom-call(f32[256,512]{1,0:T(8,128)S(1)} %convert_reduce_fusion.sum_ref, s32[1,512]{1,0:T(1,128)S(1)} %bitcast.9, s32[1,512]{1,0:T(1,128)S(1)} %bitcast.10, bf16[512,512]{1,0:T(8,128)(2,1)S(1)} %whole_green.1.refs_0_, bf16[512,512]{1,0:T(8,128)(2,1)S(1)} %collective-permute-done.1.refs_1_, ...), custom_call_target="tpu_custom_call" | custom-call | flops 400000000 | bytes 1600000 | tf_op jit(solution)/shard_map/sigma/sigma_cells/pallas_call | solution.py:166
  51.1 10.6 %all-to-all-start = ((f32[256,1,8]{2,1,0:T(1,128)}), f32[256,1,8]{2,1,0:T(1,128)S(1)}, u32[]{:S(2)}, u32[]{:S(2)}) async-start(f32[256,1,8]{2,1,0:T(1,128)} %bitcast.6), calls=%async_computation | async-start | bytes 262144 | tf_op jit(solution)/shard_map/sigma/all_to_all | solution.py:273
  61.7 0.0 copy-done.1
  61.7 0.0 copy-done.2
  61.7 0.0 copy-done.3
  61.7 7.4 %chi_terms.3 = bf16[4,256,512]{2,1,0:T(8,128)(2,1)} custom-call(bf16[512,512]{1,0:T(8,128)(2,1)} %copy-done.1, bf16[512,512]{1,0:T(8,128)(2,1)} %copy-done.2, bf16[512,512]{1,0:T(8,128)(2,1)} %copy-done.3, bf16[4,512,512]{2,1,0:T(8,128)(2,1)} %refs_3_.1, f32[4,256,512]{2,1,0:T(8,128)} %copy-done.7), custom_call_target="tpu_custom_call" | custom-call | flops 3221225472 | bytes 5767168 | tf_op jit(solution)/shard_map/chi/chi_terms/pallas_call | solution.py:205
  69.2 5.6 %all-to-all-done = f32[256,1,8]{2,1,0:T(1,128)S(1)} async-done(((f32[256,1,8]{2,1,0:T(1,128)}), f32[256,1,8]{2,1,0:T(1,128)S(1)}, u32[]{:S(2)}, u32[]{:S(2)}) %all-to-all-start) | async-done | bytes 8224 | tf_op jit(solution)/shard_map/sigma/all_to_all | solution.py:273
  74.8 0.6 reduce_sum.19
Async XLA Ops:
  1.3 10.0 %copy-start.4 = (bf16[4,512,512]{2,1,0:T(8,128)(2,1)S(1)}, bf16[4,512,512]{2,1,0:T(8,128)(2,1)}, u32[]{:S(2)}) copy-start(bf16[4,512,512]{2,1,0:T(8,128)(2,1)} %refs_3_.1) | copy-start | bytes 6291460
  7.4 14.8 %copy-start = (f32[512,512]{1,0:T(8,128)S(1)}, f32[512,512]{1,0:T(8,128)}, u32[]{:S(2)}) copy-start(f32[512,512]{1,0:T(8,128)} %get-tuple-element.12.exact_ref) | copy-start | bytes 3145732
  7.4 14.7 %collective-permute-start = (bf16[512,512]{1,0:T(8,128)(2,1)}, bf16[512,512]{1,0:T(8,128)(2,1)}, u32[]{:S(2)}, u32[]{:S(2)}) collective-permute-start(bf16[512,512]{1,0:T(8,128)(2,1)} %get-tuple-element.13), channel_id=1, source_target_pairs={{0,1},{1,0},{2,3},{3,2},{4,5},{5,4},{6,7},{7,6},{8,9},{9,8},{10,11... | collective-permute-start | bytes 1572872 | tf_op jit(solution)/shard_map/green/ppermute | solution.py:239
  23.3 24.9 %copy-start.5 = (s32[512]{0:T(512)S(1)}, s32[512]{0:T(512)}, u32[]{:S(2)}) copy-start(s32[512]{0:T(512)} %param.12) | copy-start | bytes 6148
  23.3 24.9 %copy-start.6 = (s32[512]{0:T(512)S(1)}, s32[512]{0:T(512)}, u32[]{:S(2)}) copy-start(s32[512]{0:T(512)} %param.13) | copy-start | bytes 6148
  23.3 11.2 %collective-permute-start.1 = (bf16[512,512]{1,0:T(8,128)(2,1)S(1)}, bf16[512,512]{1,0:T(8,128)(2,1)S(1)}, u32[]{:S(2)}, u32[]{:S(2)}) collective-permute-start(bf16[512,512]{1,0:T(8,128)(2,1)S(1)} %whole_green.1.refs_0_), channel_id=1, source_target_pairs={{0,2},{1,3},{2,0},{3,1},{4,6},{5,7},{6,4},{7,5},{8,10},{9,11},{10,... | collective-permute-start | bytes 1572872 | tf_op jit(solution)/shard_map/window/ppermute | solution.py:239
  25.7 15.3 %collective-permute-start.2 = (bf16[512,512]{1,0:T(8,128)(2,1)S(1)}, bf16[512,512]{1,0:T(8,128)(2,1)S(1)}, u32[]{:S(2)}, u32[]{:S(2)}) collective-permute-start(bf16[512,512]{1,0:T(8,128)(2,1)S(1)} %whole_green.1.refs_0_), channel_id=1, source_target_pairs={{0,252},{1,253},{2,6},{3,7},{4,0},{5,1},{6,10},{7,11},{8,4},{9,5},... | collective-permute-start | bytes 1572872 | tf_op jit(solution)/shard_map/window/ppermute | solution.py:239
  27.4 19.2 %collective-permute-start.3 = (bf16[512,512]{1,0:T(8,128)(2,1)S(1)}, bf16[512,512]{1,0:T(8,128)(2,1)S(1)}, u32[]{:S(2)}, u32[]{:S(2)}) collective-permute-start(bf16[512,512]{1,0:T(8,128)(2,1)S(1)} %whole_green.1.refs_0_), channel_id=1, source_target_pairs={{0,4},{1,5},{2,254},{3,255},{4,8},{5,9},{6,2},{7,3},{8,12},{9,13},... | collective-permute-start | bytes 1572872 | tf_op jit(solution)/shard_map/window/ppermute | solution.py:239
  37.7 1.3 %copy-start.7 = (f32[4,256,512]{2,1,0:T(8,128)}, f32[4,256,512]{2,1,0:T(8,128)S(1)}, u32[]{:S(2)}) copy-start(f32[4,256,512]{2,1,0:T(8,128)S(1)} %chi_terms.2.refs_4_) | copy-start | bytes 6291460
  41.1 20.6 %copy-start.1 = (bf16[512,512]{1,0:T(8,128)(2,1)}, bf16[512,512]{1,0:T(8,128)(2,1)S(1)}, u32[]{:S(2)}) copy-start(bf16[512,512]{1,0:T(8,128)(2,1)S(1)} %collective-permute-done.2.refs_2_.refs_0_) | copy-start | bytes 1572868
  41.1 7.1 %collective-permute-start.4 = (bf16[512,512]{1,0:T(8,128)(2,1)S(1)}, bf16[512,512]{1,0:T(8,128)(2,1)S(1)}, u32[]{:S(2)}, u32[]{:S(2)}) collective-permute-start(bf16[512,512]{1,0:T(8,128)(2,1)S(1)} %collective-permute-done.2.refs_2_.refs_0_), channel_id=1, source_target_pairs={{0,2},{1,3},{2,0},{3,1},{4,6},{5,7},{6,4},{7,5},{8,10},{9,11},{10,... | collective-permute-start | bytes 1572872 | tf_op jit(solution)/shard_map/window/ppermute | solution.py:239
  46.7 15.1 %copy-start.2 = (bf16[512,512]{1,0:T(8,128)(2,1)}, bf16[512,512]{1,0:T(8,128)(2,1)S(1)}, u32[]{:S(2)}) copy-start(bf16[512,512]{1,0:T(8,128)(2,1)S(1)} %collective-permute-done.3.refs_3_.refs_1_) | copy-start | bytes 1572868
  48.2 13.5 %copy-start.3 = (bf16[512,512]{1,0:T(8,128)(2,1)}, bf16[512,512]{1,0:T(8,128)(2,1)S(1)}, u32[]{:S(2)}) copy-start(bf16[512,512]{1,0:T(8,128)(2,1)S(1)} %collective-permute-done.4.refs_4_.refs_2_) | copy-start | bytes 1572868
  51.1 23.7 %all-to-all-start = ((f32[256,1,8]{2,1,0:T(1,128)}), f32[256,1,8]{2,1,0:T(1,128)S(1)}, u32[]{:S(2)}, u32[]{:S(2)}) async-start(f32[256,1,8]{2,1,0:T(1,128)} %bitcast.6), calls=%async_computation | async-start | bytes 262144 | tf_op jit(solution)/shard_map/sigma/all_to_all | solution.py:273

commit v2 on v1

--- a/solution.py
+++ b/solution.py
@@ -17,14 +17,13 @@
 MIB = 1024 * 1024
 
 
-def split_dot(left, right, dims):
-    def halves(value):
-        high = value.astype(BF16)
-        return high, (value - high.astype(F32)).astype(BF16)
-
-    (a_high, a_low), (b_high, b_low) = halves(left), halves(right)
-    dot = functools.partial(lax.dot_general, dimension_numbers=(dims, ((), ())), preferred_element_type=F32)
-    return dot(a_high, b_high) + dot(a_high, b_low) + dot(a_low, b_high)
+def split_rows(value):
+    high = value.astype(BF16)
+    return jnp.concatenate([high, (value - high.astype(F32)).astype(BF16)], axis=0)
+
+
+def across(left, right):
+    return lax.dot_general(left, right, (((1,), (1,)), ((), ())), preferred_element_type=F32)
 
 
 def partial_kernel(
@@ -96,14 +95,14 @@
             pltpu.VMEM((height, states), F32),
             pltpu.SemaphoreType.DMA((2 * CHUNKS + 1,)),
         ],
-        compiler_params=pltpu.CompilerParams(vmem_limit_bytes=60 * MIB),
+        compiler_params=pltpu.CompilerParams(vmem_limit_bytes=24 * MIB),
         cost_estimate=pl.CostEstimate(
             flops=2 * height * states * (breadth + states),
             bytes_accessed=2 * (height * breadth + breadth * states + height * states),
             transcendentals=0,
         ),
         name="partial_green",
-    )(order, vertex, right, left)
+    )(order, *[pltpu.with_memory_space_constraint(x, pltpu.HBM) for x in (vertex, right, left)])
 
 
 def green_kernel(exact_ref, got_ref, green_ref):
@@ -125,58 +124,67 @@
     )(exact, got)
 
 
-def sigma_kernel(factor, walkers, sum_ref, mom_ref, freq_ref, *refs):
-    greens, (out_ref, stacked, left, right) = refs[:walkers], refs[walkers:]
-    half, states = sum_ref.shape
-    pick_mom = (lax.broadcasted_iota(jnp.int32, (NMOM, states), 0) == mom_ref[...]).astype(BF16)
-    pick_freq = (lax.broadcasted_iota(jnp.int32, (NFREQ, states), 0) == freq_ref[...]).astype(BF16)
-    first = pl.multiple_of(lax.axis_index("pair") * half, half)
-    for u, ref in enumerate(greens):
-        stacked[u * NMOM : (u + 1) * NMOM, :] = jnp.dot(
-            pick_mom, ref[:, pl.ds(first, half)], preferred_element_type=F32
-        )
-        right[:, u * states : (u + 1) * states] = jnp.dot(
-            pick_freq, ref[...], preferred_element_type=F32
-        )
-    folded = split_dot(stacked[...], sum_ref[...], ((1,), (0,)))
-    for u in range(walkers):
-        left[:, u * states : (u + 1) * states] = folded[u * NMOM : (u + 1) * NMOM]
-    cells = split_dot(left[...], right[...], ((1,), (1,)))
-    owners, width = out_ref.shape
+def fold_walker(green, pick_mom, pick_freq, tile_sum):
+    rows, width = pick_mom.shape[0], pick_freq.shape[0]
+    by_mom = split_rows(jnp.dot(pick_mom, green, preferred_element_type=F32))
+    both = jnp.dot(by_mom, tile_sum, preferred_element_type=F32)
+    folded = split_rows(both[:rows] + both[rows:])
+    by_freq = split_rows(jnp.dot(pick_freq, green, preferred_element_type=F32))
+    terms = across(folded, by_freq)
+    terms = terms[:rows] + terms[rows:]
+    return terms[:, :width] + terms[:, width:]
+
+
+def picks(mom_ref, freq_ref, rows, width):
+    states = mom_ref.shape[1]
+    per_row = rows // NMOM
+    mom = lax.broadcasted_iota(jnp.int32, (rows, states), 0) // per_row == mom_ref[...]
+    freq = lax.broadcasted_iota(jnp.int32, (width, states), 0) == freq_ref[...]
+    return mom.astype(F32).astype(BF16), freq.astype(F32).astype(BF16)
+
+
+def own_kernel(green_ref, sum_ref, mom_ref, freq_ref, out_ref):
+    pick_mom, pick_freq = picks(mom_ref, freq_ref, *out_ref.shape)
+    out_ref[...] = fold_walker(green_ref[...], pick_mom, pick_freq, sum_ref[...])
+
+
+def sigma_kernel(factor, cells_ref, in_ref, far_ref, chip_ref, own_ref, mom_ref, freq_ref, out_ref):
+    pick_mom, pick_freq = picks(mom_ref, freq_ref, *cells_ref.shape)
+    cells = (
+        cells_ref[...]
+        + fold_walker(in_ref[...], pick_mom, pick_freq, chip_ref[...])
+        + fold_walker(far_ref[...], pick_mom, pick_freq, own_ref[...])
+    ) * factor
+    rows, width = out_ref.shape
+    owner = lax.broadcasted_iota(jnp.int32, (rows, width), 0) * lax.axis_size(
+        "pair"
+    ) + lax.axis_index("pair")
     fold = NFREQ // width
-    owner = lax.broadcasted_iota(jnp.int32, (owners, NMOM), 0)
-    column = lax.broadcasted_iota(jnp.int32, (owners, NMOM), 1)
-    spread = jnp.dot(
-        (owner // fold == column).astype(F32),
-        cells * factor,
-        precision=lax.Precision.HIGHEST,
-        preferred_element_type=F32,
-    )
-    turn = lax.broadcasted_iota(jnp.int32, (owners, width), 0) % fold
-    result = jnp.zeros((owners, width), F32)
+    result = jnp.zeros((rows, width), F32)
     for part in range(fold):
-        result = jnp.where(turn == part, spread[:, part * width : (part + 1) * width], result)
+        result = jnp.where(
+            owner % fold == part, cells[:, part * width : (part + 1) * width], result
+        )
     out_ref[...] = result
 
 
-def sigma_cells(factor, tile_sum, greens, momentum, frequency, owners):
-    width = NMOM * NFREQ // owners
-    states = tile_sum.shape[1]
+def small_call(kernel, shape, flops, name):
     vmem = pl.BlockSpec(memory_space=pltpu.VMEM)
-    return pl.pallas_call(
-        functools.partial(sigma_kernel, factor, len(greens)),
-        in_specs=[vmem] * (3 + len(greens)),
-        out_specs=vmem,
-        out_shape=jax.ShapeDtypeStruct((owners, width), F32),
-        scratch_shapes=[
-            pltpu.VMEM((len(greens) * NMOM, states // 2), F32),
-            pltpu.VMEM((NMOM, len(greens) * states), F32),
-            pltpu.VMEM((NFREQ, len(greens) * states), F32),
-        ],
-        compiler_params=pltpu.CompilerParams(vmem_limit_bytes=16 * MIB),
-        cost_estimate=pl.CostEstimate(flops=400_000_000, bytes_accessed=1_600_000, transcendentals=0),
-        name="sigma_cells",
-    )(tile_sum, momentum[None, :], frequency[None, :], *greens)
+
+    def call(*operands):
+        return pl.pallas_call(
+            kernel,
+            in_specs=[vmem] * len(operands),
+            out_specs=vmem,
+            out_shape=jax.ShapeDtypeStruct(shape, F32),
+            compiler_params=pltpu.CompilerParams(vmem_limit_bytes=16 * MIB),
+            cost_estimate=pl.CostEstimate(
+                flops=flops, bytes_accessed=sum(2 * x.size for x in operands), transcendentals=0
+            ),
+            name=name,
+        )(*operands)
+
+    return call
 
 
 def chi_kernel(walkers, scale, *refs):
@@ -217,7 +225,7 @@
             transcendentals=0,
         ),
         name="chi_terms",
-    )(*greens, tiles, *extra)
+    )(*greens, tiles, *[pltpu.with_memory_space_constraint(x, pltpu.HBM) for x in extra])
 
 
 def moves(mesh_shape):
@@ -247,33 +255,42 @@
 
     with jax.named_scope("green"):
         exact, sent = partial_green(orders, vertex[0], right_phase[0], left_phase[0])
+        sent, later_tiles = lax.optimization_barrier((sent, tiles))
         received = send(sent, other)
-        own_rows = lax.dynamic_slice_in_dim(tiles, lax.axis_index("pair") * half, half, 1)
-        tile_sum = jnp.sum(own_rows.astype(F32), axis=0)
-        received, tile_sum = lax.optimization_barrier((received, tile_sum))
+        own_sum = jnp.sum(later_tiles.astype(F32), axis=0)
+        sent_sum = own_sum.astype(BF16)
+        chip_sum = (own_sum + send(sent_sum, core).astype(F32)).astype(BF16)
+        received, sent_sum, chip_sum = lax.optimization_barrier((received, sent_sum, chip_sum))
         green = whole_green(exact, received)
 
     with jax.named_scope("window"):
+        mom, freq = momentum[None, :], frequency[None, :]
         green_core = send(green, core)
         green_in = send(green, inward)
         green_out = send(green, outward)
         running = chi_terms([green, green_core], tiles, None, 1.0, F32, 24)
-        running, green_in = lax.optimization_barrier((running, green_in))
+        cells = small_call(own_kernel, (blk, NFREQ), 200_000_000, "own_cells")(
+            green, chip_sum, mom, freq
+        )
+        running, cells, green_in = lax.optimization_barrier((running, cells, green_in))
         green_last = send(green_in, core)
-        far = [green_in, green_out, green_last]
 
     with jax.named_scope("sigma"):
         factor = 1.0 / math.sqrt(
             5.0 * tiles.shape[0] * blk * states * states / (NMOM * NFREQ)
         ) / math.sqrt(states)
-        cells = sigma_cells(
-            factor, tile_sum, [green, green_core] + far, momentum, frequency, blk * pair
-        )
+        cells = small_call(
+            functools.partial(sigma_kernel, factor),
+            (blk, NMOM * NFREQ // (blk * pair)),
+            400_000_000,
+            "sigma_cells",
+        )(cells, green_in, green_out, chip_sum, sent_sum, mom, freq)
         running, cells = lax.optimization_barrier((running, cells))
-        spread = lax.all_to_all(cells, BOTH, 0, 0, tiled=True)
+        spread = lax.all_to_all(cells, "blk", 0, 0, tiled=True)
 
     with jax.named_scope("chi"):
-        suscept = chi_terms(far, tiles, running, 1.0 / math.sqrt(states), BF16, 60)
+        far = [green_in, green_out, green_last]
+        suscept = chi_terms(far, tiles, running, 1.0 / math.sqrt(states), BF16, 24)
         suscept, spread = lax.optimization_barrier((suscept, spread))
         owned = jnp.sum(spread, axis=0)
     return suscept, owned

time: 75.6 us -> 68.3 us (0.903)
  starting transfers between devices: 31.2 us -> 27.5 us
  Pallas kernels: 20.8 us -> 18.3 us
  local copies, waits for them, and re-layouts: 1.36 us -> 0.02 us
    ppermute x5 -> x6, starting transfers between devices: 20.6 us -> 18.1 us  [send(): return lax.ppermute(value, BOTH, pairs)]
    all_to_all x1, waiting for transfers between devices: 5.61 us -> 3.75 us  [per_device(): spread = lax.all_to_all(cells, 'blk', 0, 0, tiled=True)]
    ppermute x5 -> x6, waiting for transfers between devices: 14.3 us -> 16.1 us  [send(): return lax.ppermute(value, BOTH, pairs)]
    unnamed x16 -> x8, local copies, waits for them, and re-layouts: 1.36 us -> 0.02 us
    all_to_all x1, starting transfers between devices: 10.6 us -> 9.43 us  [per_device(): spread = lax.all_to_all(cells, 'blk', 0, 0, tiled=True)]
    pallas_call x1, Pallas kernels: 6.14 us -> 5.01 us  [partial_green(): pl.pallas_call(functools.partial(partial_kernel, 1.0 / math.sqrt(breadth)...]
    pallas_call x1, Pallas kernels: 1.13 us -> 0.09 us  [whole_green(): pl.pallas_call(green_kernel, in_specs=[vmem] * 2, out_specs=vmem, out_sha...]
    pallas_call x1 -> x2, Pallas kernels: 2.92 us -> 3.12 us  [call(): pl.pallas_call(kernel, in_specs=[vmem] * len(operands), out_specs=vmem, o...]
  transfers between devices with their start and end apart: 6 -> 7, of which waited for: 4 -> 4; matrix products, arithmetic and copies ran while one was open for 0% -> 0% of each run, Pallas kernels for 14% -> 19%
where the time goes in v2:
time: 68.3 us; the launch traced here: 68.1 us
  starting transfers between devices  27.5 us (40%)
  waiting for transfers between devices  19.9 us (29%)
  Pallas kernels  18.3 us (27%)
  between operations  1.39 us (2%)
  other arithmetic  1.09 us (2%)
    ppermute x6, starting transfers between devices, send(): return lax.ppermute(value, BOTH, pairs)  18.1 us
    ppermute x6, waiting for transfers between devices, send(): return lax.ppermute(value, BOTH, pairs)  16.1 us
    pallas_call x2, Pallas kernels, chi_terms(): pl.pallas_call(functools.partial(chi_kernel, len(greens), scale), grid=(c...  10.1 us
    all_to_all x1, starting transfers between devices, per_device(): spread = lax.all_to_all(cells, 'blk', 0, 0, tiled=True)  9.43 us
    pallas_call x1, Pallas kernels, partial_green(): pl.pallas_call(functools.partial(partial_kernel, 1.0 / math.sqrt(breadth)...  5.01 us
    all_to_all x1, waiting for transfers between devices, per_device(): spread = lax.all_to_all(cells, 'blk', 0, 0, tiled=True)  3.75 us
    pallas_call x2, Pallas kernels, call(): pl.pallas_call(kernel, in_specs=[vmem] * len(operands), out_specs=vmem, o...  3.12 us
  transfers between devices with their start and end apart: 7, of which 4 were waited for; matrix products, arithmetic and copies ran while one was open for 0% of the time, Pallas kernels for 19%

profile of v2, /device:TPU:1, one launch (start us, length us, event | category | flops | bytes accessed | tf_op | source)
XLA Modules:
  0.0 68.1 jit_solution(16496698001897367720)
XLA Ops:
  1.3 0.0 copy-start
  1.3 5.0 %partial_green.1 = (f32[512,512]{1,0:T(8,128)S(1)}, bf16[512,512]{1,0:T(8,128)(2,1)S(1)}) custom-call(s32[1]{0:T(128)S(6)} %copy.10.order_ref, bf16[1024,2048]{1,0:T(8,128)(2,1)} %bitcast.14, bf16[2048,512]{1,0:T(8,128)(2,1)} %bitcast.15, bf16[1024,512]{1,0:T(8,128)(2,1)} %bitcast.16), custom_call_target="tpu_custom_call" | custom-call | flops 2684354560 | bytes 7340032 | tf_op jit(solution)/shard_map/green/partial_green/pallas_call | solution.py:83
  6.3 0.0 copy-done
  6.3 0.3 convert_reduce_fusion
  6.6 0.1 convert_element_type.13.own_ref
  6.7 0.0 copy-start.1
  6.7 0.0 copy-start.2
  6.7 3.2 %collective-permute-start.1 = (bf16[512,512]{1,0:T(8,128)(2,1)S(1)}, bf16[512,512]{1,0:T(8,128)(2,1)S(1)}, u32[]{:S(2)}, u32[]{:S(2)}) collective-permute-start(bf16[512,512]{1,0:T(8,128)(2,1)S(1)} %convert_element_type.13.own_ref), channel_id=1, source_target_pairs={{0,2},{1,3},{2,0},{3,1},{4,6},{5,7},{6,4},{7,5},{8,10},{9,11},{10,... | collective-permute-start | bytes 1572872 | tf_op jit(solution)/shard_map/green/ppermute | solution.py:247
  9.9 1.2 %collective-permute-start = (bf16[512,512]{1,0:T(8,128)(2,1)S(1)}, bf16[512,512]{1,0:T(8,128)(2,1)S(1)}, u32[]{:S(2)}, u32[]{:S(2)}) collective-permute-start(bf16[512,512]{1,0:T(8,128)(2,1)S(1)} %get-tuple-element.18), channel_id=1, source_target_pairs={{0,1},{1,0},{2,3},{3,2},{4,5},{5,4},{6,7},{7,6},{8,9},{9,8},{10,11... | collective-permute-start | bytes 1572872 | tf_op jit(solution)/shard_map/green/ppermute | solution.py:247
  11.1 0.3 collective-permute-done.1
  11.5 0.2 add_convert_fusion.sum_ref.chip_ref
  11.7 13.3 %collective-permute-done.got_ref = bf16[512,512]{1,0:T(8,128)(2,1)S(1)} collective-permute-done((bf16[512,512]{1,0:T(8,128)(2,1)S(1)}, bf16[512,512]{1,0:T(8,128)(2,1)S(1)}, u32[]{:S(2)}, u32[]{:S(2)}) %collective-permute-start) | collective-permute-done | bytes 524320 | tf_op jit(solution)/shard_map/green/ppermute | solution.py:247
  24.9 0.1 whole_green.1.refs_0_.green_ref
  25.0 1.0 %collective-permute-start.2 = (bf16[512,512]{1,0:T(8,128)(2,1)S(1)}, bf16[512,512]{1,0:T(8,128)(2,1)S(1)}, u32[]{:S(2)}, u32[]{:S(2)}) collective-permute-start(bf16[512,512]{1,0:T(8,128)(2,1)S(1)} %whole_green.1.refs_0_.green_ref), channel_id=1, source_target_pairs={{0,2},{1,3},{2,0},{3,1},{4,6},{5,7},{6,4},{7,5},{8,10},{9,11},{10,... | collective-permute-start | bytes 1572872 | tf_op jit(solution)/shard_map/window/ppermute | solution.py:247
  26.0 0.0 collective-permute-start.3
  26.0 7.1 %collective-permute-start.4 = (bf16[512,512]{1,0:T(8,128)(2,1)S(1)}, bf16[512,512]{1,0:T(8,128)(2,1)S(1)}, u32[]{:S(2)}, u32[]{:S(2)}) collective-permute-start(bf16[512,512]{1,0:T(8,128)(2,1)S(1)} %whole_green.1.refs_0_.green_ref), channel_id=1, source_target_pairs={{0,4},{1,5},{2,254},{3,255},{4,8},{5,9},{6,2},{7,3},{8,12},{9,13},... | collective-permute-start | bytes 1572872 | tf_op jit(solution)/shard_map/window/ppermute | solution.py:247
  33.1 0.0 copy-done.1
  33.1 0.0 copy-done.2
  33.1 0.8 %own_cells.1.cells_ref = f32[128,32]{1,0:T(8,128)S(1)} custom-call(bf16[512,512]{1,0:T(8,128)(2,1)S(1)} %whole_green.1.refs_0_.green_ref, bf16[512,512]{1,0:T(8,128)(2,1)S(1)} %add_convert_fusion.sum_ref.chip_ref, s32[1,512]{1,0:T(1,128)S(1)} %bitcast.9, s32[1,512]{1,0:T(1,128)S(1)} %bitcast.11), custom_call_target="tpu_custom_call" | custom-call | flops 200000000 | bytes 1050624 | tf_op jit(solution)/shard_map/window/own_cells/pallas_call | solution.py:175
  34.0 0.0 collective-permute-done.2.refs_1_
  34.0 3.2 %chi_terms.2.refs_4_ = f32[4,256,512]{2,1,0:T(8,128)S(1)} custom-call(bf16[512,512]{1,0:T(8,128)(2,1)S(1)} %whole_green.1.refs_0_.green_ref, bf16[512,512]{1,0:T(8,128)(2,1)S(1)} %collective-permute-done.2.refs_1_, bf16[4,512,512]{2,1,0:T(8,128)(2,1)S(1)} %copy-done), custom_call_target="tpu_custom_call" | custom-call | flops 2147483648 | bytes 5242880 | tf_op jit(solution)/shard_map/window/chi_terms/pallas_call | solution.py:213
  37.2 0.0 copy-start.3
  37.2 2.5 %collective-permute-done.3.in_ref.refs_0_ = bf16[512,512]{1,0:T(8,128)(2,1)S(1)} collective-permute-done((bf16[512,512]{1,0:T(8,128)(2,1)S(1)}, bf16[512,512]{1,0:T(8,128)(2,1)S(1)}, u32[]{:S(2)}, u32[]{:S(2)}) %collective-permute-start.3) | collective-permute-done | bytes 524320 | tf_op jit(solution)/shard_map/window/ppermute | solution.py:247
  39.7 5.6 %collective-permute-start.5 = (bf16[512,512]{1,0:T(8,128)(2,1)S(1)}, bf16[512,512]{1,0:T(8,128)(2,1)}, u32[]{:S(2)}, u32[]{:S(2)}) collective-permute-start(bf16[512,512]{1,0:T(8,128)(2,1)S(1)} %collective-permute-done.3.in_ref.refs_0_), channel_id=1, source_target_pairs={{0,2},{1,3},{2,0},{3,1},{4,6},{5,7},{6,4},{7,5},{8,10},{9,11},{10,... | collective-permute-start | bytes 1572872 | tf_op jit(solution)/shard_map/window/ppermute | solution.py:247
  45.2 0.0 collective-permute-done.4.far_ref.refs_1_
  45.2 2.3 %sigma_cells.1 = f32[128,8]{1,0:T(8,128)} custom-call(f32[128,32]{1,0:T(8,128)S(1)} %own_cells.1.cells_ref, bf16[512,512]{1,0:T(8,128)(2,1)S(1)} %collective-permute-done.3.in_ref.refs_0_, bf16[512,512]{1,0:T(8,128)(2,1)S(1)} %collective-permute-done.4.far_ref.refs_1_, bf16[512,512]{1,0:T(8,128)(2,1)S(1)} %add_convert_fusion.sum_ref.chip_ref, ...), custom_call_target="tpu_custom_call" | custom-call | flops 400000000 | bytes 2107392 | tf_op jit(solution)/shard_map/sigma/sigma_cells/pallas_call | solution.py:175
  47.5 0.0 copy-done.3
  47.5 9.4 %all-to-all-start = ((f32[128,1,8]{2,1,0:T(1,128)}), f32[128,1,8]{2,1,0:T(1,128)S(1)}, u32[]{:S(2)}, u32[]{:S(2)}) async-start(f32[128,1,8]{2,1,0:T(1,128)} %bitcast.6), calls=%async_computation | async-start | bytes 131072 | tf_op jit(solution)/shard_map/sigma/all_to_all | solution.py:289
  57.0 0.0 collective-permute-done.5.refs_2_
  57.0 6.9 %chi_terms.3 = bf16[4,256,512]{2,1,0:T(8,128)(2,1)} custom-call(bf16[512,512]{1,0:T(8,128)(2,1)S(1)} %collective-permute-done.3.in_ref.refs_0_, bf16[512,512]{1,0:T(8,128)(2,1)S(1)} %collective-permute-done.4.far_ref.refs_1_, bf16[512,512]{1,0:T(8,128)(2,1)} %collective-permute-done.5.refs_2_, bf16[4,512,512]{2,1,0:T(8,128)(2,1)S(1)} %copy-done, ...), custom_call_target="tpu_custom_call" | custom-call | flops 3221225472 | bytes 5767168 | tf_op jit(solution)/shard_map/chi/chi_terms/pallas_call | solution.py:213
  63.9 3.8 %all-to-all-done = f32[128,1,8]{2,1,0:T(1,128)S(1)} async-done(((f32[128,1,8]{2,1,0:T(1,128)}), f32[128,1,8]{2,1,0:T(1,128)S(1)}, u32[]{:S(2)}, u32[]{:S(2)}) %all-to-all-start) | async-done | bytes 4128 | tf_op jit(solution)/shard_map/sigma/all_to_all | solution.py:289
  67.6 0.5 reduce_sum.19
Async XLA Ops:
  1.3 5.0 %copy-start = (bf16[4,512,512]{2,1,0:T(8,128)(2,1)S(1)}, bf16[4,512,512]{2,1,0:T(8,128)(2,1)}, u32[]{:S(2)}) copy-start(bf16[4,512,512]{2,1,0:T(8,128)(2,1)} %refs_3_.1) | copy-start | bytes 6291460
  6.7 26.4 %copy-start.1 = (s32[512]{0:T(512)S(1)}, s32[512]{0:T(512)}, u32[]{:S(2)}) copy-start(s32[512]{0:T(512)} %param.12) | copy-start | bytes 6148
  6.7 26.4 %copy-start.2 = (s32[512]{0:T(512)S(1)}, s32[512]{0:T(512)}, u32[]{:S(2)}) copy-start(s32[512]{0:T(512)} %param.13) | copy-start | bytes 6148
  6.7 4.7 %collective-permute-start.1 = (bf16[512,512]{1,0:T(8,128)(2,1)S(1)}, bf16[512,512]{1,0:T(8,128)(2,1)S(1)}, u32[]{:S(2)}, u32[]{:S(2)}) collective-permute-start(bf16[512,512]{1,0:T(8,128)(2,1)S(1)} %convert_element_type.13.own_ref), channel_id=1, source_target_pairs={{0,2},{1,3},{2,0},{3,1},{4,6},{5,7},{6,4},{7,5},{8,10},{9,11},{10,... | collective-permute-start | bytes 1572872 | tf_op jit(solution)/shard_map/green/ppermute | solution.py:247
  9.9 15.0 %collective-permute-start = (bf16[512,512]{1,0:T(8,128)(2,1)S(1)}, bf16[512,512]{1,0:T(8,128)(2,1)S(1)}, u32[]{:S(2)}, u32[]{:S(2)}) collective-permute-start(bf16[512,512]{1,0:T(8,128)(2,1)S(1)} %get-tuple-element.18), channel_id=1, source_target_pairs={{0,1},{1,0},{2,3},{3,2},{4,5},{5,4},{6,7},{7,6},{8,9},{9,8},{10,11... | collective-permute-start | bytes 1572872 | tf_op jit(solution)/shard_map/green/ppermute | solution.py:247
  25.0 8.9 %collective-permute-start.2 = (bf16[512,512]{1,0:T(8,128)(2,1)S(1)}, bf16[512,512]{1,0:T(8,128)(2,1)S(1)}, u32[]{:S(2)}, u32[]{:S(2)}) collective-permute-start(bf16[512,512]{1,0:T(8,128)(2,1)S(1)} %whole_green.1.refs_0_.green_ref), channel_id=1, source_target_pairs={{0,2},{1,3},{2,0},{3,1},{4,6},{5,7},{6,4},{7,5},{8,10},{9,11},{10,... | collective-permute-start | bytes 1572872 | tf_op jit(solution)/shard_map/window/ppermute | solution.py:247
  26.0 13.7 %collective-permute-start.3 = (bf16[512,512]{1,0:T(8,128)(2,1)S(1)}, bf16[512,512]{1,0:T(8,128)(2,1)S(1)}, u32[]{:S(2)}, u32[]{:S(2)}) collective-permute-start(bf16[512,512]{1,0:T(8,128)(2,1)S(1)} %whole_green.1.refs_0_.green_ref), channel_id=1, source_target_pairs={{0,252},{1,253},{2,6},{3,7},{4,0},{5,1},{6,10},{7,11},{8,4},{9,5},... | collective-permute-start | bytes 1572872 | tf_op jit(solution)/shard_map/window/ppermute | solution.py:247
  26.0 19.3 %collective-permute-start.4 = (bf16[512,512]{1,0:T(8,128)(2,1)S(1)}, bf16[512,512]{1,0:T(8,128)(2,1)S(1)}, u32[]{:S(2)}, u32[]{:S(2)}) collective-permute-start(bf16[512,512]{1,0:T(8,128)(2,1)S(1)} %whole_green.1.refs_0_.green_ref), channel_id=1, source_target_pairs={{0,4},{1,5},{2,254},{3,255},{4,8},{5,9},{6,2},{7,3},{8,12},{9,13},... | collective-permute-start | bytes 1572872 | tf_op jit(solution)/shard_map/window/ppermute | solution.py:247
  37.2 10.4 %copy-start.3 = (f32[4,256,512]{2,1,0:T(8,128)}, f32[4,256,512]{2,1,0:T(8,128)S(1)}, u32[]{:S(2)}) copy-start(f32[4,256,512]{2,1,0:T(8,128)S(1)} %chi_terms.2.refs_4_) | copy-start | bytes 6291460
  39.7 17.3 %collective-permute-start.5 = (bf16[512,512]{1,0:T(8,128)(2,1)S(1)}, bf16[512,512]{1,0:T(8,128)(2,1)}, u32[]{:S(2)}, u32[]{:S(2)}) collective-permute-start(bf16[512,512]{1,0:T(8,128)(2,1)S(1)} %collective-permute-done.3.in_ref.refs_0_), channel_id=1, source_target_pairs={{0,2},{1,3},{2,0},{3,1},{4,6},{5,7},{6,4},{7,5},{8,10},{9,11},{10,... | collective-permute-start | bytes 1572872 | tf_op jit(solution)/shard_map/window/ppermute | solution.py:247
  47.5 20.1 %all-to-all-start = ((f32[128,1,8]{2,1,0:T(1,128)}), f32[128,1,8]{2,1,0:T(1,128)S(1)}, u32[]{:S(2)}, u32[]{:S(2)}) async-start(f32[128,1,8]{2,1,0:T(1,128)} %bitcast.6), calls=%async_computation | async-start | bytes 131072 | tf_op jit(solution)/shard_map/sigma/all_to_all | solution.py:289

commit v3 on v2

--- a/solution.py
+++ b/solution.py
@@ -126,10 +126,13 @@
 
 def fold_walker(green, pick_mom, pick_freq, tile_sum):
     rows, width = pick_mom.shape[0], pick_freq.shape[0]
-    by_mom = split_rows(jnp.dot(pick_mom, green, preferred_element_type=F32))
+    picked = jnp.dot(
+        jnp.concatenate([pick_mom, pick_freq], axis=0), green, preferred_element_type=F32
+    )
+    by_mom = split_rows(picked[:rows])
     both = jnp.dot(by_mom, tile_sum, preferred_element_type=F32)
     folded = split_rows(both[:rows] + both[rows:])
-    by_freq = split_rows(jnp.dot(pick_freq, green, preferred_element_type=F32))
+    by_freq = split_rows(picked[rows:])
     terms = across(folded, by_freq)
     terms = terms[:rows] + terms[rows:]
     return terms[:, :width] + terms[:, width:]
@@ -143,17 +146,18 @@
     return mom.astype(F32).astype(BF16), freq.astype(F32).astype(BF16)
 
 
-def own_kernel(green_ref, sum_ref, mom_ref, freq_ref, out_ref):
+def own_kernel(green_ref, sums_ref, mom_ref, freq_ref, out_ref):
     pick_mom, pick_freq = picks(mom_ref, freq_ref, *out_ref.shape)
-    out_ref[...] = fold_walker(green_ref[...], pick_mom, pick_freq, sum_ref[...])
-
-
-def sigma_kernel(factor, cells_ref, in_ref, far_ref, chip_ref, own_ref, mom_ref, freq_ref, out_ref):
+    out_ref[...] = fold_walker(green_ref[...], pick_mom, pick_freq, sums_ref[1])
+
+
+def sigma_kernel(factor, cells_ref, below_ref, above_ref, sums_ref, mom_ref, freq_ref, out_ref, last_ref):
     pick_mom, pick_freq = picks(mom_ref, freq_ref, *cells_ref.shape)
+    upper = lax.axis_index("blk") % 2
     cells = (
         cells_ref[...]
-        + fold_walker(in_ref[...], pick_mom, pick_freq, chip_ref[...])
-        + fold_walker(far_ref[...], pick_mom, pick_freq, own_ref[...])
+        + fold_walker(below_ref[...], pick_mom, pick_freq, sums_ref[upper])
+        + fold_walker(above_ref[...], pick_mom, pick_freq, sums_ref[1 - upper])
     ) * factor
     rows, width = out_ref.shape
     owner = lax.broadcasted_iota(jnp.int32, (rows, width), 0) * lax.axis_size(
@@ -167,6 +171,14 @@
         )
     out_ref[...] = result
 
+    @pl.when(upper == 1)
+    def _():
+        last_ref[...] = below_ref[...]
+
+    @pl.when(upper == 0)
+    def _():
+        last_ref[...] = above_ref[...]
+
 
 def small_call(kernel, shape, flops, name):
     vmem = pl.BlockSpec(memory_space=pltpu.VMEM)
@@ -175,8 +187,8 @@
         return pl.pallas_call(
             kernel,
             in_specs=[vmem] * len(operands),
-            out_specs=vmem,
-            out_shape=jax.ShapeDtypeStruct(shape, F32),
+            out_specs=jax.tree.map(lambda _: vmem, shape),
+            out_shape=shape,
             compiler_params=pltpu.CompilerParams(vmem_limit_bytes=16 * MIB),
             cost_estimate=pl.CostEstimate(
                 flops=flops, bytes_accessed=sum(2 * x.size for x in operands), transcendentals=0
@@ -240,7 +252,7 @@
     def along(even, odd):
         return flat(lambda b, p: ((b + (odd if b % 2 else even)) % blk) * pair + p)
 
-    return other, core, along(2, -2), along(-2, 2)
+    return other, core, along(2, 2), along(-2, -2)
 
 
 def send(value, pairs):
@@ -251,45 +263,50 @@
     states = right_phase.shape[2]
     half = states // 2
     blk, pair = lax.axis_size("blk"), lax.axis_size("pair")
-    other, core, outward, inward = moves((blk, pair))
+    other, core, upward, downward = moves((blk, pair))
 
     with jax.named_scope("green"):
         exact, sent = partial_green(orders, vertex[0], right_phase[0], left_phase[0])
-        sent, later_tiles = lax.optimization_barrier((sent, tiles))
         received = send(sent, other)
+        green = whole_green(exact, received)
+
+    with jax.named_scope("tile_sums"):
+        green, later_tiles = lax.optimization_barrier((green, tiles))
         own_sum = jnp.sum(later_tiles.astype(F32), axis=0)
-        sent_sum = own_sum.astype(BF16)
-        chip_sum = (own_sum + send(sent_sum, core).astype(F32)).astype(BF16)
-        received, sent_sum, chip_sum = lax.optimization_barrier((received, sent_sum, chip_sum))
-        green = whole_green(exact, received)
+        own_short = own_sum.astype(BF16)
+        chip_sum = (own_sum + send(own_short, core).astype(F32)).astype(BF16)
+        sums = jnp.stack([own_short, chip_sum])
 
     with jax.named_scope("window"):
         mom, freq = momentum[None, :], frequency[None, :]
         green_core = send(green, core)
-        green_in = send(green, inward)
-        green_out = send(green, outward)
+        below = send(green, upward)
+        above = send(green, downward)
         running = chi_terms([green, green_core], tiles, None, 1.0, F32, 24)
-        cells = small_call(own_kernel, (blk, NFREQ), 200_000_000, "own_cells")(
-            green, chip_sum, mom, freq
-        )
-        running, cells, green_in = lax.optimization_barrier((running, cells, green_in))
-        green_last = send(green_in, core)
+        cells = small_call(
+            own_kernel, jax.ShapeDtypeStruct((blk, NFREQ), F32), 200_000_000, "own_cells"
+        )(green, sums, mom, freq)
+        running, cells, below, above = lax.optimization_barrier((running, cells, below, above))
 
     with jax.named_scope("sigma"):
         factor = 1.0 / math.sqrt(
             5.0 * tiles.shape[0] * blk * states * states / (NMOM * NFREQ)
         ) / math.sqrt(states)
-        cells = small_call(
+        cells, last = small_call(
             functools.partial(sigma_kernel, factor),
-            (blk, NMOM * NFREQ // (blk * pair)),
+            [
+                jax.ShapeDtypeStruct((blk, NMOM * NFREQ // (blk * pair)), F32),
+                jax.ShapeDtypeStruct(green.shape, BF16),
+            ],
             400_000_000,
             "sigma_cells",
-        )(cells, green_in, green_out, chip_sum, sent_sum, mom, freq)
-        running, cells = lax.optimization_barrier((running, cells))
+        )(cells, below, above, sums, mom, freq)
+        running, cells, last = lax.optimization_barrier((running, cells, last))
+        green_last = send(last, core)
         spread = lax.all_to_all(cells, "blk", 0, 0, tiled=True)
 
     with jax.named_scope("chi"):
-        far = [green_in, green_out, green_last]
+        far = [below, above, green_last]
         suscept = chi_terms(far, tiles, running, 1.0 / math.sqrt(states), BF16, 24)
         suscept, spread = lax.optimization_barrier((suscept, spread))
         owned = jnp.sum(spread, axis=0)

time: 68.3 us -> 67.8 us (level)
  starting transfers between devices: 27.5 us -> 25.1 us
  waiting for transfers between devices: 19.9 us -> 21.8 us
    ppermute x6, waiting for transfers between devices: 16.1 us -> 18.1 us  [send(): return lax.ppermute(value, BOTH, pairs)]
    ppermute x6, starting transfers between devices: 18.1 us -> 16.4 us  [send(): return lax.ppermute(value, BOTH, pairs)]
  transfers between devices with their start and end apart: 7 -> 7, of which waited for: 4 -> 3; matrix products, arithmetic and copies ran while one was open for 0% -> 0% of each run, Pallas kernels for 19% -> 16%
where the time goes in v3:
time: 67.8 us; the launch traced here: 67.5 us
  starting transfers between devices  25.1 us (37%)
  waiting for transfers between devices  21.8 us (32%)
  Pallas kernels  17.9 us (26%)
  between operations  1.42 us (2%)
  other arithmetic  1.26 us (2%)
    ppermute x6, waiting for transfers between devices, send(): return lax.ppermute(value, BOTH, pairs)  18.1 us
    ppermute x6, starting transfers between devices, send(): return lax.ppermute(value, BOTH, pairs)  16.4 us
    pallas_call x2, Pallas kernels, chi_terms(): pl.pallas_call(functools.partial(chi_kernel, len(greens), scale), grid=(c...  10.1 us
    all_to_all x1, starting transfers between devices, per_device(): spread = lax.all_to_all(cells, 'blk', 0, 0, tiled=True)  8.77 us
    pallas_call x1, Pallas kernels, partial_green(): pl.pallas_call(functools.partial(partial_kernel, 1.0 / math.sqrt(breadth)...  4.69 us
    all_to_all x1, waiting for transfers between devices, per_device(): spread = lax.all_to_all(cells, 'blk', 0, 0, tiled=True)  3.72 us
    pallas_call x2, Pallas kernels, call(): pl.pallas_call(kernel, in_specs=[vmem] * len(operands), out_specs=jax.tre...  3.03 us
  transfers between devices with their start and end apart: 7, of which 3 were waited for; matrix products, arithmetic and copies ran while one was open for 0% of the time, Pallas kernels for 16%

profile of v3, /device:TPU:1, one launch (start us, length us, event | category | flops | bytes accessed | tf_op | source)
XLA Modules:
  0.0 67.5 jit_solution(15084841519023959254)
XLA Ops:
  1.3 4.7 %partial_green.1 = (f32[512,512]{1,0:T(8,128)S(1)}, bf16[512,512]{1,0:T(8,128)(2,1)S(1)}) custom-call(s32[1]{0:T(128)S(6)} %copy.10.order_ref, bf16[1024,2048]{1,0:T(8,128)(2,1)} %bitcast.18, bf16[2048,512]{1,0:T(8,128)(2,1)} %bitcast.19, bf16[1024,512]{1,0:T(8,128)(2,1)} %bitcast.20), custom_call_target="tpu_custom_call" | custom-call | flops 2684354560 | bytes 7340032 | tf_op jit(solution)/shard_map/green/partial_green/pallas_call | solution.py:83
  6.0 0.0 copy-start
  6.0 3.8 %collective-permute-start = (bf16[512,512]{1,0:T(8,128)(2,1)S(1)}, bf16[512,512]{1,0:T(8,128)(2,1)S(1)}, u32[]{:S(2)}, u32[]{:S(2)}) collective-permute-start(bf16[512,512]{1,0:T(8,128)(2,1)S(1)} %get-tuple-element.18), channel_id=1, source_target_pairs={{0,1},{1,0},{2,3},{3,2},{4,5},{5,4},{6,7},{7,6},{8,9},{9,8},{10,11... | collective-permute-start | bytes 1572872 | tf_op jit(solution)/shard_map/green/ppermute | solution.py:259
  9.8 10.5 %collective-permute-done.got_ref = bf16[512,512]{1,0:T(8,128)(2,1)S(1)} collective-permute-done((bf16[512,512]{1,0:T(8,128)(2,1)S(1)}, bf16[512,512]{1,0:T(8,128)(2,1)S(1)}, u32[]{:S(2)}, u32[]{:S(2)}) %collective-permute-start) | collective-permute-done | bytes 524320 | tf_op jit(solution)/shard_map/green/ppermute | solution.py:259
  20.3 0.1 whole_green.1.refs_0_.green_ref
  20.4 0.0 copy-done
  20.5 0.3 convert_reduce_fusion
  20.8 0.1 convert_element_type.23
  20.8 2.4 %collective-permute-start.2 = (bf16[512,512]{1,0:T(8,128)(2,1)S(1)}, bf16[512,512]{1,0:T(8,128)(2,1)S(1)}, u32[]{:S(2)}, u32[]{:S(2)}) collective-permute-start(bf16[512,512]{1,0:T(8,128)(2,1)S(1)} %convert_element_type.23), channel_id=1, source_target_pairs={{0,2},{1,3},{2,0},{3,1},{4,6},{5,7},{6,4},{7,5},{8,10},{9,11},{10,... | collective-permute-start | bytes 1572872 | tf_op jit(solution)/shard_map/tile_sums/ppermute | solution.py:259
  23.3 0.1 collective-permute-start.1
  23.4 0.1 convert_bitcast_fusion
  23.5 0.0 copy-start.1
  23.5 0.0 copy-start.2
  23.5 1.8 %collective-permute-start.3 = (bf16[512,512]{1,0:T(8,128)(2,1)S(1)}, bf16[512,512]{1,0:T(8,128)(2,1)S(1)}, u32[]{:S(2)}, u32[]{:S(2)}) collective-permute-start(bf16[512,512]{1,0:T(8,128)(2,1)S(1)} %whole_green.1.refs_0_.green_ref), channel_id=1, source_target_pairs={{0,4},{1,5},{2,6},{3,7},{4,8},{5,9},{6,10},{7,11},{8,12},{9,13},{1... | collective-permute-start | bytes 1572872 | tf_op jit(solution)/shard_map/window/ppermute | solution.py:259
  25.3 7.2 %collective-permute-start.4 = (bf16[512,512]{1,0:T(8,128)(2,1)S(1)}, bf16[512,512]{1,0:T(8,128)(2,1)S(1)}, u32[]{:S(2)}, u32[]{:S(2)}) collective-permute-start(bf16[512,512]{1,0:T(8,128)(2,1)S(1)} %whole_green.1.refs_0_.green_ref), channel_id=1, source_target_pairs={{0,252},{1,253},{2,254},{3,255},{4,0},{5,1},{6,2},{7,3},{8,4},{9,5... | collective-permute-start | bytes 1572872 | tf_op jit(solution)/shard_map/window/ppermute | solution.py:259
  32.5 0.0 collective-permute-done.2
  32.5 0.2 fusion
  32.7 0.1 pad_maximum_fusion.sums_ref
  32.8 0.0 copy-done.1
  32.8 0.0 copy-done.2
  32.8 0.8 %own_cells.1.cells_ref = f32[128,32]{1,0:T(8,128)S(1)} custom-call(bf16[512,512]{1,0:T(8,128)(2,1)S(1)} %whole_green.1.refs_0_.green_ref, bf16[2,512,512]{2,1,0:T(8,128)(2,1)S(1)} %pad_maximum_fusion.sums_ref, s32[1,512]{1,0:T(1,128)S(1)} %bitcast.13, s32[1,512]{1,0:T(1,128)S(1)} %bitcast.15), custom_call_target="tpu_custom_call" | custom-call | flops 200000000 | bytes 1574912 | tf_op jit(solution)/shard_map/window/own_cells/pallas_call | solution.py:187
  33.6 0.0 collective-permute-done.1.refs_1_
  33.6 3.2 %chi_terms.2.refs_4_ = f32[4,256,512]{2,1,0:T(8,128)S(1)} custom-call(bf16[512,512]{1,0:T(8,128)(2,1)S(1)} %whole_green.1.refs_0_.green_ref, bf16[512,512]{1,0:T(8,128)(2,1)S(1)} %collective-permute-done.1.refs_1_, bf16[4,512,512]{2,1,0:T(8,128)(2,1)S(1)} %copy-done), custom_call_target="tpu_custom_call" | custom-call | flops 2147483648 | bytes 5242880 | tf_op jit(solution)/shard_map/window/chi_terms/pallas_call | solution.py:225
  36.8 0.0 copy-start.3
  36.8 7.6 %collective-permute-done.3.below_ref.refs_0_ = bf16[512,512]{1,0:T(8,128)(2,1)S(1)} collective-permute-done((bf16[512,512]{1,0:T(8,128)(2,1)S(1)}, bf16[512,512]{1,0:T(8,128)(2,1)S(1)}, u32[]{:S(2)}, u32[]{:S(2)}) %collective-permute-start.3) | collective-permute-done | bytes 524320 | tf_op jit(solution)/shard_map/window/ppermute | solution.py:259
  44.4 0.0 collective-permute-done.4.above_ref.refs_1_
  44.4 2.3 %sigma_cells.1 = (f32[128,8]{1,0:T(8,128)}, bf16[512,512]{1,0:T(8,128)(2,1)}) custom-call(f32[128,32]{1,0:T(8,128)S(1)} %own_cells.1.cells_ref, bf16[512,512]{1,0:T(8,128)(2,1)S(1)} %collective-permute-done.3.below_ref.refs_0_, bf16[512,512]{1,0:T(8,128)(2,1)S(1)} %collective-permute-done.4.above_ref.refs_1_, ...), custom_call_target="tpu_custom_call" | custom-call | flops 400000000 | bytes 2107392 | tf_op jit(solution)/shard_map/sigma/sigma_cells/pallas_call | solution.py:187
  46.6 0.0 copy-done.3
  46.6 1.0 %collective-permute-start.5 = (bf16[512,512]{1,0:T(8,128)(2,1)}, bf16[512,512]{1,0:T(8,128)(2,1)}, u32[]{:S(2)}, u32[]{:S(2)}) collective-permute-start(bf16[512,512]{1,0:T(8,128)(2,1)} %get-tuple-element.27), channel_id=1, source_target_pairs={{0,2},{1,3},{2,0},{3,1},{4,6},{5,7},{6,4},{7,5},{8,10},{9,11},{10,... | collective-permute-start | bytes 1572872 | tf_op jit(solution)/shard_map/sigma/ppermute | solution.py:259
  47.6 8.8 %all-to-all-start = ((f32[128,1,8]{2,1,0:T(1,128)}), f32[128,1,8]{2,1,0:T(1,128)S(1)}, u32[]{:S(2)}, u32[]{:S(2)}) async-start(f32[128,1,8]{2,1,0:T(1,128)} %bitcast.8), calls=%async_computation | async-start | bytes 131072 | tf_op jit(solution)/shard_map/sigma/all_to_all | solution.py:306
  56.4 0.0 collective-permute-done.5.refs_2_
  56.4 6.9 %chi_terms.3 = bf16[4,256,512]{2,1,0:T(8,128)(2,1)} custom-call(bf16[512,512]{1,0:T(8,128)(2,1)S(1)} %collective-permute-done.3.below_ref.refs_0_, bf16[512,512]{1,0:T(8,128)(2,1)S(1)} %collective-permute-done.4.above_ref.refs_1_, bf16[512,512]{1,0:T(8,128)(2,1)} %collective-permute-done.5.refs_2_, bf16[4,512,512]{2,1,0:T(8,128)(2,1)S(1)} %copy-done, ...), custom_call_target="tpu_custom_call" | custom-call | flops 3221225472 | bytes 5767168 | tf_op jit(solution)/shard_map/chi/chi_terms/pallas_call | solution.py:225
  63.3 3.7 %all-to-all-done = f32[128,1,8]{2,1,0:T(1,128)S(1)} async-done(((f32[128,1,8]{2,1,0:T(1,128)}), f32[128,1,8]{2,1,0:T(1,128)S(1)}, u32[]{:S(2)}, u32[]{:S(2)}) %all-to-all-start) | async-done | bytes 4128 | tf_op jit(solution)/shard_map/sigma/all_to_all | solution.py:306
  67.0 0.5 reduce_sum.19
Async XLA Ops:
  6.0 14.5 %copy-start = (bf16[4,512,512]{2,1,0:T(8,128)(2,1)S(1)}, bf16[4,512,512]{2,1,0:T(8,128)(2,1)}, u32[]{:S(2)}) copy-start(bf16[4,512,512]{2,1,0:T(8,128)(2,1)} %refs_3_.1) | copy-start | bytes 6291460
  6.0 14.4 %collective-permute-start = (bf16[512,512]{1,0:T(8,128)(2,1)S(1)}, bf16[512,512]{1,0:T(8,128)(2,1)S(1)}, u32[]{:S(2)}, u32[]{:S(2)}) collective-permute-start(bf16[512,512]{1,0:T(8,128)(2,1)S(1)} %get-tuple-element.18), channel_id=1, source_target_pairs={{0,1},{1,0},{2,3},{3,2},{4,5},{5,4},{6,7},{7,6},{8,9},{9,8},{10,11... | collective-permute-start | bytes 1572872 | tf_op jit(solution)/shard_map/green/ppermute | solution.py:259
  20.8 11.7 %collective-permute-start.2 = (bf16[512,512]{1,0:T(8,128)(2,1)S(1)}, bf16[512,512]{1,0:T(8,128)(2,1)S(1)}, u32[]{:S(2)}, u32[]{:S(2)}) collective-permute-start(bf16[512,512]{1,0:T(8,128)(2,1)S(1)} %convert_element_type.23), channel_id=1, source_target_pairs={{0,2},{1,3},{2,0},{3,1},{4,6},{5,7},{6,4},{7,5},{8,10},{9,11},{10,... | collective-permute-start | bytes 1572872 | tf_op jit(solution)/shard_map/tile_sums/ppermute | solution.py:259
  23.3 10.3 %collective-permute-start.1 = (bf16[512,512]{1,0:T(8,128)(2,1)S(1)}, bf16[512,512]{1,0:T(8,128)(2,1)S(1)}, u32[]{:S(2)}, u32[]{:S(2)}) collective-permute-start(bf16[512,512]{1,0:T(8,128)(2,1)S(1)} %whole_green.1.refs_0_.green_ref), channel_id=1, source_target_pairs={{0,2},{1,3},{2,0},{3,1},{4,6},{5,7},{6,4},{7,5},{8,10},{9,11},{10,... | collective-permute-start | bytes 1572872 | tf_op jit(solution)/shard_map/window/ppermute | solution.py:259
  23.5 9.4 %copy-start.1 = (s32[512]{0:T(512)S(1)}, s32[512]{0:T(512)}, u32[]{:S(2)}) copy-start(s32[512]{0:T(512)} %param.12) | copy-start | bytes 6148
  23.5 9.4 %copy-start.2 = (s32[512]{0:T(512)S(1)}, s32[512]{0:T(512)}, u32[]{:S(2)}) copy-start(s32[512]{0:T(512)} %param.13) | copy-start | bytes 6148
  23.5 20.9 %collective-permute-start.3 = (bf16[512,512]{1,0:T(8,128)(2,1)S(1)}, bf16[512,512]{1,0:T(8,128)(2,1)S(1)}, u32[]{:S(2)}, u32[]{:S(2)}) collective-permute-start(bf16[512,512]{1,0:T(8,128)(2,1)S(1)} %whole_green.1.refs_0_.green_ref), channel_id=1, source_target_pairs={{0,4},{1,5},{2,6},{3,7},{4,8},{5,9},{6,10},{7,11},{8,12},{9,13},{1... | collective-permute-start | bytes 1572872 | tf_op jit(solution)/shard_map/window/ppermute | solution.py:259
  25.3 19.1 %collective-permute-start.4 = (bf16[512,512]{1,0:T(8,128)(2,1)S(1)}, bf16[512,512]{1,0:T(8,128)(2,1)S(1)}, u32[]{:S(2)}, u32[]{:S(2)}) collective-permute-start(bf16[512,512]{1,0:T(8,128)(2,1)S(1)} %whole_green.1.refs_0_.green_ref), channel_id=1, source_target_pairs={{0,252},{1,253},{2,254},{3,255},{4,0},{5,1},{6,2},{7,3},{8,4},{9,5... | collective-permute-start | bytes 1572872 | tf_op jit(solution)/shard_map/window/ppermute | solution.py:259
  36.8 9.8 %copy-start.3 = (f32[4,256,512]{2,1,0:T(8,128)}, f32[4,256,512]{2,1,0:T(8,128)S(1)}, u32[]{:S(2)}) copy-start(f32[4,256,512]{2,1,0:T(8,128)S(1)} %chi_terms.2.refs_4_) | copy-start | bytes 6291460
  46.6 9.7 %collective-permute-start.5 = (bf16[512,512]{1,0:T(8,128)(2,1)}, bf16[512,512]{1,0:T(8,128)(2,1)}, u32[]{:S(2)}, u32[]{:S(2)}) collective-permute-start(bf16[512,512]{1,0:T(8,128)(2,1)} %get-tuple-element.27), channel_id=1, source_target_pairs={{0,2},{1,3},{2,0},{3,1},{4,6},{5,7},{6,4},{7,5},{8,10},{9,11},{10,... | collective-permute-start | bytes 1572872 | tf_op jit(solution)/shard_map/sigma/ppermute | solution.py:259
  47.6 19.4 %all-to-all-start = ((f32[128,1,8]{2,1,0:T(1,128)}), f32[128,1,8]{2,1,0:T(1,128)S(1)}, u32[]{:S(2)}, u32[]{:S(2)}) async-start(f32[128,1,8]{2,1,0:T(1,128)} %bitcast.8), calls=%async_computation | async-start | bytes 131072 | tf_op jit(solution)/shard_map/sigma/all_to_all | solution.py:306

commit v4 on v3

--- a/solution.py
+++ b/solution.py
@@ -13,7 +13,7 @@
 BOTH = ("blk", "pair")
 F32 = jnp.float32
 BF16 = jnp.bfloat16
-CHUNKS = 4
+CHUNKS = 8
 MIB = 1024 * 1024
 
 

time: 67.8 us -> 67.7 us (level)
  no operation moved by 1% of the time
where the time goes in v4:
time: 67.7 us; the launch traced here: 67.6 us
  starting transfers between devices  24.9 us (37%)
  waiting for transfers between devices  21.9 us (32%)
  Pallas kernels  18 us (27%)
  between operations  1.42 us (2%)
  other arithmetic  1.26 us (2%)
    ppermute x6, waiting for transfers between devices, send(): return lax.ppermute(value, BOTH, pairs)  18.2 us
    ppermute x6, starting transfers between devices, send(): return lax.ppermute(value, BOTH, pairs)  16.1 us
    pallas_call x2, Pallas kernels, chi_terms(): pl.pallas_call(functools.partial(chi_kernel, len(greens), scale), grid=(c...  10.1 us
    all_to_all x1, starting transfers between devices, per_device(): spread = lax.all_to_all(cells, 'blk', 0, 0, tiled=True)  8.78 us
    pallas_call x1, Pallas kernels, partial_green(): pl.pallas_call(functools.partial(partial_kernel, 1.0 / math.sqrt(breadth)...  4.84 us
    all_to_all x1, waiting for transfers between devices, per_device(): spread = lax.all_to_all(cells, 'blk', 0, 0, tiled=True)  3.72 us
    pallas_call x2, Pallas kernels, call(): pl.pallas_call(kernel, in_specs=[vmem] * len(operands), out_specs=jax.tre...  3.02 us
  transfers between devices with their start and end apart: 7, of which 3 were waited for; matrix products, arithmetic and copies ran while one was open for 0% of the time, Pallas kernels for 16%

profile of v4, /device:TPU:1, one launch (start us, length us, event | category | flops | bytes accessed | tf_op | source)
XLA Modules:
  0.0 67.6 jit_solution(16399754636193651351)
XLA Ops:
  1.3 4.8 %partial_green.1 = (f32[512,512]{1,0:T(8,128)S(1)}, bf16[512,512]{1,0:T(8,128)(2,1)S(1)}) custom-call(s32[1]{0:T(128)S(6)} %copy.10.order_ref, bf16[1024,2048]{1,0:T(8,128)(2,1)} %bitcast.18, bf16[2048,512]{1,0:T(8,128)(2,1)} %bitcast.19, bf16[1024,512]{1,0:T(8,128)(2,1)} %bitcast.20), custom_call_target="tpu_custom_call" | custom-call | flops 2684354560 | bytes 7340032 | tf_op jit(solution)/shard_map/green/partial_green/pallas_call | solution.py:83
  6.1 0.0 copy-start
  6.1 3.9 %collective-permute-start = (bf16[512,512]{1,0:T(8,128)(2,1)S(1)}, bf16[512,512]{1,0:T(8,128)(2,1)S(1)}, u32[]{:S(2)}, u32[]{:S(2)}) collective-permute-start(bf16[512,512]{1,0:T(8,128)(2,1)S(1)} %get-tuple-element.18), channel_id=1, source_target_pairs={{0,1},{1,0},{2,3},{3,2},{4,5},{5,4},{6,7},{7,6},{8,9},{9,8},{10,11... | collective-permute-start | bytes 1572872 | tf_op jit(solution)/shard_map/green/ppermute | solution.py:259
  10.0 10.6 %collective-permute-done.got_ref = bf16[512,512]{1,0:T(8,128)(2,1)S(1)} collective-permute-done((bf16[512,512]{1,0:T(8,128)(2,1)S(1)}, bf16[512,512]{1,0:T(8,128)(2,1)S(1)}, u32[]{:S(2)}, u32[]{:S(2)}) %collective-permute-start) | collective-permute-done | bytes 524320 | tf_op jit(solution)/shard_map/green/ppermute | solution.py:259
  20.6 0.1 whole_green.1.refs_0_.green_ref
  20.7 0.0 copy-done
  20.7 0.3 convert_reduce_fusion
  21.1 0.1 convert_element_type.23
  21.1 2.3 %collective-permute-start.2 = (bf16[512,512]{1,0:T(8,128)(2,1)S(1)}, bf16[512,512]{1,0:T(8,128)(2,1)S(1)}, u32[]{:S(2)}, u32[]{:S(2)}) collective-permute-start(bf16[512,512]{1,0:T(8,128)(2,1)S(1)} %convert_element_type.23), channel_id=1, source_target_pairs={{0,2},{1,3},{2,0},{3,1},{4,6},{5,7},{6,4},{7,5},{8,10},{9,11},{10,... | collective-permute-start | bytes 1572872 | tf_op jit(solution)/shard_map/tile_sums/ppermute | solution.py:259
  23.5 0.1 collective-permute-start.1
  23.6 0.1 convert_bitcast_fusion
  23.6 0.0 copy-start.1
  23.6 0.0 copy-start.2
  23.7 1.8 %collective-permute-start.3 = (bf16[512,512]{1,0:T(8,128)(2,1)S(1)}, bf16[512,512]{1,0:T(8,128)(2,1)S(1)}, u32[]{:S(2)}, u32[]{:S(2)}) collective-permute-start(bf16[512,512]{1,0:T(8,128)(2,1)S(1)} %whole_green.1.refs_0_.green_ref), channel_id=1, source_target_pairs={{0,4},{1,5},{2,6},{3,7},{4,8},{5,9},{6,10},{7,11},{8,12},{9,13},{1... | collective-permute-start | bytes 1572872 | tf_op jit(solution)/shard_map/window/ppermute | solution.py:259
  25.4 7.1 %collective-permute-start.4 = (bf16[512,512]{1,0:T(8,128)(2,1)S(1)}, bf16[512,512]{1,0:T(8,128)(2,1)S(1)}, u32[]{:S(2)}, u32[]{:S(2)}) collective-permute-start(bf16[512,512]{1,0:T(8,128)(2,1)S(1)} %whole_green.1.refs_0_.green_ref), channel_id=1, source_target_pairs={{0,252},{1,253},{2,254},{3,255},{4,0},{5,1},{6,2},{7,3},{8,4},{9,5... | collective-permute-start | bytes 1572872 | tf_op jit(solution)/shard_map/window/ppermute | solution.py:259
  32.5 0.0 collective-permute-done.2
  32.6 0.2 fusion
  32.7 0.1 pad_maximum_fusion.sums_ref
  32.8 0.0 copy-done.1
  32.8 0.0 copy-done.2
  32.8 0.8 %own_cells.1.cells_ref = f32[128,32]{1,0:T(8,128)S(1)} custom-call(bf16[512,512]{1,0:T(8,128)(2,1)S(1)} %whole_green.1.refs_0_.green_ref, bf16[2,512,512]{2,1,0:T(8,128)(2,1)S(1)} %pad_maximum_fusion.sums_ref, s32[1,512]{1,0:T(1,128)S(1)} %bitcast.13, s32[1,512]{1,0:T(1,128)S(1)} %bitcast.15), custom_call_target="tpu_custom_call" | custom-call | flops 200000000 | bytes 1574912 | tf_op jit(solution)/shard_map/window/own_cells/pallas_call | solution.py:187
  33.6 0.0 collective-permute-done.1.refs_1_
  33.6 3.2 %chi_terms.2.refs_4_ = f32[4,256,512]{2,1,0:T(8,128)S(1)} custom-call(bf16[512,512]{1,0:T(8,128)(2,1)S(1)} %whole_green.1.refs_0_.green_ref, bf16[512,512]{1,0:T(8,128)(2,1)S(1)} %collective-permute-done.1.refs_1_, bf16[4,512,512]{2,1,0:T(8,128)(2,1)S(1)} %copy-done), custom_call_target="tpu_custom_call" | custom-call | flops 2147483648 | bytes 5242880 | tf_op jit(solution)/shard_map/window/chi_terms/pallas_call | solution.py:225
  36.8 0.0 copy-start.3
  36.8 7.6 %collective-permute-done.3.below_ref.refs_0_ = bf16[512,512]{1,0:T(8,128)(2,1)S(1)} collective-permute-done((bf16[512,512]{1,0:T(8,128)(2,1)S(1)}, bf16[512,512]{1,0:T(8,128)(2,1)S(1)}, u32[]{:S(2)}, u32[]{:S(2)}) %collective-permute-start.3) | collective-permute-done | bytes 524320 | tf_op jit(solution)/shard_map/window/ppermute | solution.py:259
  44.4 0.0 collective-permute-done.4.above_ref.refs_1_
  44.4 2.2 %sigma_cells.1 = (f32[128,8]{1,0:T(8,128)}, bf16[512,512]{1,0:T(8,128)(2,1)}) custom-call(f32[128,32]{1,0:T(8,128)S(1)} %own_cells.1.cells_ref, bf16[512,512]{1,0:T(8,128)(2,1)S(1)} %collective-permute-done.3.below_ref.refs_0_, bf16[512,512]{1,0:T(8,128)(2,1)S(1)} %collective-permute-done.4.above_ref.refs_1_, ...), custom_call_target="tpu_custom_call" | custom-call | flops 400000000 | bytes 2107392 | tf_op jit(solution)/shard_map/sigma/sigma_cells/pallas_call | solution.py:187
  46.7 0.0 copy-done.3
  46.7 1.0 %collective-permute-start.5 = (bf16[512,512]{1,0:T(8,128)(2,1)}, bf16[512,512]{1,0:T(8,128)(2,1)}, u32[]{:S(2)}, u32[]{:S(2)}) collective-permute-start(bf16[512,512]{1,0:T(8,128)(2,1)} %get-tuple-element.27), channel_id=1, source_target_pairs={{0,2},{1,3},{2,0},{3,1},{4,6},{5,7},{6,4},{7,5},{8,10},{9,11},{10,... | collective-permute-start | bytes 1572872 | tf_op jit(solution)/shard_map/sigma/ppermute | solution.py:259
  47.6 8.8 %all-to-all-start = ((f32[128,1,8]{2,1,0:T(1,128)}), f32[128,1,8]{2,1,0:T(1,128)S(1)}, u32[]{:S(2)}, u32[]{:S(2)}) async-start(f32[128,1,8]{2,1,0:T(1,128)} %bitcast.8), calls=%async_computation | async-start | bytes 131072 | tf_op jit(solution)/shard_map/sigma/all_to_all | solution.py:306
  56.4 0.0 collective-permute-done.5.refs_2_
  56.4 6.9 %chi_terms.3 = bf16[4,256,512]{2,1,0:T(8,128)(2,1)} custom-call(bf16[512,512]{1,0:T(8,128)(2,1)S(1)} %collective-permute-done.3.below_ref.refs_0_, bf16[512,512]{1,0:T(8,128)(2,1)S(1)} %collective-permute-done.4.above_ref.refs_1_, bf16[512,512]{1,0:T(8,128)(2,1)} %collective-permute-done.5.refs_2_, bf16[4,512,512]{2,1,0:T(8,128)(2,1)S(1)} %copy-done, ...), custom_call_target="tpu_custom_call" | custom-call | flops 3221225472 | bytes 5767168 | tf_op jit(solution)/shard_map/chi/chi_terms/pallas_call | solution.py:225
  63.3 3.7 %all-to-all-done = f32[128,1,8]{2,1,0:T(1,128)S(1)} async-done(((f32[128,1,8]{2,1,0:T(1,128)}), f32[128,1,8]{2,1,0:T(1,128)S(1)}, u32[]{:S(2)}, u32[]{:S(2)}) %all-to-all-start) | async-done | bytes 4128 | tf_op jit(solution)/shard_map/sigma/all_to_all | solution.py:306
  67.0 0.5 reduce_sum.19
Async XLA Ops:
  6.1 14.6 %copy-start = (bf16[4,512,512]{2,1,0:T(8,128)(2,1)S(1)}, bf16[4,512,512]{2,1,0:T(8,128)(2,1)}, u32[]{:S(2)}) copy-start(bf16[4,512,512]{2,1,0:T(8,128)(2,1)} %refs_3_.1) | copy-start | bytes 6291460
  6.1 14.5 %collective-permute-start = (bf16[512,512]{1,0:T(8,128)(2,1)S(1)}, bf16[512,512]{1,0:T(8,128)(2,1)S(1)}, u32[]{:S(2)}, u32[]{:S(2)}) collective-permute-start(bf16[512,512]{1,0:T(8,128)(2,1)S(1)} %get-tuple-element.18), channel_id=1, source_target_pairs={{0,1},{1,0},{2,3},{3,2},{4,5},{5,4},{6,7},{7,6},{8,9},{9,8},{10,11... | collective-permute-start | bytes 1572872 | tf_op jit(solution)/shard_map/green/ppermute | solution.py:259
  21.1 11.4 %collective-permute-start.2 = (bf16[512,512]{1,0:T(8,128)(2,1)S(1)}, bf16[512,512]{1,0:T(8,128)(2,1)S(1)}, u32[]{:S(2)}, u32[]{:S(2)}) collective-permute-start(bf16[512,512]{1,0:T(8,128)(2,1)S(1)} %convert_element_type.23), channel_id=1, source_target_pairs={{0,2},{1,3},{2,0},{3,1},{4,6},{5,7},{6,4},{7,5},{8,10},{9,11},{10,... | collective-permute-start | bytes 1572872 | tf_op jit(solution)/shard_map/tile_sums/ppermute | solution.py:259
  23.5 10.2 %collective-permute-start.1 = (bf16[512,512]{1,0:T(8,128)(2,1)S(1)}, bf16[512,512]{1,0:T(8,128)(2,1)S(1)}, u32[]{:S(2)}, u32[]{:S(2)}) collective-permute-start(bf16[512,512]{1,0:T(8,128)(2,1)S(1)} %whole_green.1.refs_0_.green_ref), channel_id=1, source_target_pairs={{0,2},{1,3},{2,0},{3,1},{4,6},{5,7},{6,4},{7,5},{8,10},{9,11},{10,... | collective-permute-start | bytes 1572872 | tf_op jit(solution)/shard_map/window/ppermute | solution.py:259
  23.6 9.2 %copy-start.1 = (s32[512]{0:T(512)S(1)}, s32[512]{0:T(512)}, u32[]{:S(2)}) copy-start(s32[512]{0:T(512)} %param.12) | copy-start | bytes 6148
  23.6 9.2 %copy-start.2 = (s32[512]{0:T(512)S(1)}, s32[512]{0:T(512)}, u32[]{:S(2)}) copy-start(s32[512]{0:T(512)} %param.13) | copy-start | bytes 6148
  23.7 20.8 %collective-permute-start.3 = (bf16[512,512]{1,0:T(8,128)(2,1)S(1)}, bf16[512,512]{1,0:T(8,128)(2,1)S(1)}, u32[]{:S(2)}, u32[]{:S(2)}) collective-permute-start(bf16[512,512]{1,0:T(8,128)(2,1)S(1)} %whole_green.1.refs_0_.green_ref), channel_id=1, source_target_pairs={{0,4},{1,5},{2,6},{3,7},{4,8},{5,9},{6,10},{7,11},{8,12},{9,13},{1... | collective-permute-start | bytes 1572872 | tf_op jit(solution)/shard_map/window/ppermute | solution.py:259
  25.4 19.0 %collective-permute-start.4 = (bf16[512,512]{1,0:T(8,128)(2,1)S(1)}, bf16[512,512]{1,0:T(8,128)(2,1)S(1)}, u32[]{:S(2)}, u32[]{:S(2)}) collective-permute-start(bf16[512,512]{1,0:T(8,128)(2,1)S(1)} %whole_green.1.refs_0_.green_ref), channel_id=1, source_target_pairs={{0,252},{1,253},{2,254},{3,255},{4,0},{5,1},{6,2},{7,3},{8,4},{9,5... | collective-permute-start | bytes 1572872 | tf_op jit(solution)/shard_map/window/ppermute | solution.py:259
  36.8 9.8 %copy-start.3 = (f32[4,256,512]{2,1,0:T(8,128)}, f32[4,256,512]{2,1,0:T(8,128)S(1)}, u32[]{:S(2)}) copy-start(f32[4,256,512]{2,1,0:T(8,128)S(1)} %chi_terms.2.refs_4_) | copy-start | bytes 6291460
  46.7 9.7 %collective-permute-start.5 = (bf16[512,512]{1,0:T(8,128)(2,1)}, bf16[512,512]{1,0:T(8,128)(2,1)}, u32[]{:S(2)}, u32[]{:S(2)}) collective-permute-start(bf16[512,512]{1,0:T(8,128)(2,1)} %get-tuple-element.27), channel_id=1, source_target_pairs={{0,2},{1,3},{2,0},{3,1},{4,6},{5,7},{6,4},{7,5},{8,10},{9,11},{10,... | collective-permute-start | bytes 1572872 | tf_op jit(solution)/shard_map/sigma/ppermute | solution.py:259
  47.6 19.4 %all-to-all-start = ((f32[128,1,8]{2,1,0:T(1,128)}), f32[128,1,8]{2,1,0:T(1,128)S(1)}, u32[]{:S(2)}, u32[]{:S(2)}) async-start(f32[128,1,8]{2,1,0:T(1,128)} %bitcast.8), calls=%async_computation | async-start | bytes 131072 | tf_op jit(solution)/shard_map/sigma/all_to_all | solution.py:306
